TPU v7x, 256 devices: a whole 4x4x8 slice. The times are simulated.
256 devices in a mesh: col: 32 (over x_hi, z, core), row: 8 (over y, x_lo).
Axes of the slice: x: 4 (x_hi: 2, x_lo: 2; x = x_hi * 2 + x_lo), y: 4, z: 8, core: 2. Of those that a mesh axis runs over, the one named last changes fastest.
Arguments:
- start_field: float32 [2, 512, 8192], P(None, 'row', 'col'), may hold values from -36 to 36
- seam_target: float32 [2, 2, 16, 65536], P(None, None, 'row', 'col'), may hold values from -6 to 6
- seam_rows: int32 [4, 16, 65536], P(None, 'row', 'col'), may hold values from 0 to 30
- seam_band: int32 [4, 16, 65536], P(None, 'row', 'col'), may hold values from 0 to 2
- seam_frac: int32 [4, 2, 16, 65536], P(None, None, 'row', 'col'), may hold values from 0 to 255
- adjacency: int32 [2, 16, 256], P(None, 'row', 'col'), may hold values 0 or 1
Outputs:
- refined_field: float32 [2, 512, 8192], P(None, 'row', 'col')
- last_residual: float32 [2, 512, 8192], P(None, 'row', 'col')
Inputs may be any that keep to these rules, and one draw needn't show every extreme that they name: `seam_rows`: index of the cell along the seam, in control points of the tile. `seam_band`: depth of the cell from the tile's edge. `seam_frac`: offsets in 256ths of a cell.
All inputs are finite; a program needn't handle non-finite values. No bound on the sum of `adjacency` on one device may be relied on, other than what follows from the above.
Results may differ from a plain program's by a relative error of at most 0.0003.
Values sent between devices are 32-bit elements; how exact they have to be, the bound alone decides.
A program may use at most 64 MiB of HBM per device.

v0:
```python
import functools

import jax
import jax.numpy as jnp
from jax import lax
from jax.experimental import pallas as pl
from jax.experimental.pallas import tpu as pltpu
from jax.sharding import PartitionSpec as P

GRID = 32
BAND = 4
ITERS = 3


BEND_WEIGHT = 0.05
DAMPING = 0.5


MESH_ID = pl.DeviceIdType.MESH


def _cg_kernel(names, first, last, d_ref, h_ref, r_ref, u_ref, rr_ref, *refs):
    if last:
        u_out, r_out, row_buf, col_buf, mine, part, row_send, row_recv, col_send, col_recv = refs
    else:
        (u_out, r_out, d_out, rr_out, row_buf, col_buf, mine, part, row_send, row_recv, col_send,
         col_recv) = refs
    ncol = lax.axis_size("col")
    nrow = lax.axis_size("row")
    ci = lax.axis_index("col")
    ri = lax.axis_index("row")

    def dev(c, r):
        where = {"col": c, "row": r}
        return tuple(where[n] for n in names)

    direction = d_ref[...]
    image = h_ref[...]
    residual = r_ref[...]

    def total(x):
        return jnp.sum(jnp.sum(x, axis=0, keepdims=True), axis=1, keepdims=True)

    parts = [total(direction * image)]
    if not last:
        parts += [total(image * image), total(residual * image)]
    if first:
        parts += [total(residual * residual)]
    lane = lax.broadcasted_iota(jnp.int32, (8, 128), 1)
    sub = lax.broadcasted_iota(jnp.int32, (8, 128), 0)
    tile = jnp.zeros((8, 128), jnp.float32)
    for k, value in enumerate(parts):
        tile = jnp.where((sub == 0) & (lane == k), value, tile)
    mine[...] = tile

    barrier = pltpu.get_barrier_semaphore()

    @pl.loop(1, nrow)
    def _(k):
        pl.semaphore_signal(barrier, 1, device_id=dev(ci, (ri + k) % nrow), device_id_type=MESH_ID)

    @pl.loop(1, ncol)
    def _(k):
        pl.semaphore_signal(barrier, 1, device_id=dev((ci + k) % ncol, ri), device_id_type=MESH_ID)

    pl.semaphore_wait(barrier, nrow - 1 + ncol - 1)

    def row_copy(peer, slot):
        return pltpu.make_async_remote_copy(
            src_ref=mine, dst_ref=row_buf.at[slot], send_sem=row_send.at[peer],
            recv_sem=row_recv.at[slot], device_id=dev(ci, peer), device_id_type=MESH_ID)

    for k in range(1, nrow):
        row_copy((ri + k) % nrow, ri).start()
    row_buf[ri] = tile
    for k in range(1, nrow):
        row_copy((ri + k) % nrow, ri).wait_send()
        peer = (ri + nrow - k) % nrow
        row_copy(peer, peer).wait_recv()
    summed = row_buf[0]
    for j in range(1, nrow):
        summed = summed + row_buf[j]
    part[...] = summed

    def col_copy(peer, slot):
        return pltpu.make_async_remote_copy(
            src_ref=part, dst_ref=col_buf.at[slot], send_sem=col_send.at[peer],
            recv_sem=col_recv.at[slot], device_id=dev(peer, ri), device_id_type=MESH_ID)

    @pl.loop(1, ncol)
    def _(k):
        col_copy((ci + k) % ncol, ci).start()

    col_buf[ci] = summed

    @pl.loop(1, ncol)
    def _(k):
        col_copy((ci + k) % ncol, ci).wait_send()
        peer = (ci + ncol - k) % ncol
        col_copy(peer, peer).wait_recv()

    summed = lax.fori_loop(1, ncol, lambda j, acc: acc + col_buf[j], col_buf[0])

    def pick(k):
        return jnp.sum(jnp.where((sub == 0) & (lane == k), summed, 0.0), axis=(0, 1), keepdims=True)

    curv = pick(0)
    norm_now = pick(len(parts) - 1) if first else rr_ref[0:1, 0:1]
    step_size = norm_now / curv
    u_out[...] = u_ref[...] + step_size * direction
    residual = residual - step_size * image
    r_out[...] = residual
    if not last:
        image_sq = pick(1)
        cross = curv if first else pick(2)
        norm_next = norm_now - 2.0 * step_size * cross + step_size * step_size * image_sq
        d_out[...] = residual + norm_next / norm_now * direction
        rr_out[...] = jnp.broadcast_to(norm_next, (8, 128))


def cg_step(names, iteration, direction, image, residual, update, norm_tile):
    ncol = lax.axis_size("col")
    nrow = lax.axis_size("row")
    first = iteration == 0
    last = iteration == ITERS - 1
    shape = direction.shape
    flat = (shape[0] * shape[1], shape[2])
    fields = [x.reshape(flat) for x in (direction, image, residual, update)]
    field_type = jax.ShapeDtypeStruct(flat, jnp.float32)
    out_shape = [field_type, field_type]
    if not last:
        out_shape += [field_type, jax.ShapeDtypeStruct((8, 128), jnp.float32)]
    got = pl.pallas_call(
        functools.partial(_cg_kernel, names, first, last),
        out_shape=tuple(out_shape),
        in_specs=[pl.BlockSpec(memory_space=pltpu.VMEM)] * 5,
        out_specs=tuple(pl.BlockSpec(memory_space=pltpu.VMEM) for _ in out_shape),
        scratch_shapes=[
            pltpu.VMEM((nrow, 8, 128), jnp.float32),
            pltpu.VMEM((ncol, 8, 128), jnp.float32),
            pltpu.VMEM((8, 128), jnp.float32),
            pltpu.VMEM((8, 128), jnp.float32),
            pltpu.SemaphoreType.DMA((nrow,)),
            pltpu.SemaphoreType.DMA((nrow,)),
            pltpu.SemaphoreType.DMA((ncol,)),
            pltpu.SemaphoreType.DMA((ncol,)),
        ],
        compiler_params=pltpu.CompilerParams(
            collective_id=10 + iteration, has_side_effects=True
        ),
    )(*fields, norm_tile)
    update = got[0].reshape(shape)
    residual = got[1].reshape(shape)
    if last:
        return update, residual, None, None
    return update, residual, got[2].reshape(shape), got[3]


def tile_view(control, tile_rows, tile_cols, points):
    return control.reshape(2, tile_rows, points, tile_cols, points)


def edge_band(tile_grid, facing, band_depth):
    if facing == 0:
        return tile_grid[..., ::-1][..., :band_depth].transpose(0, 1, 3, 2, 4)
    if facing == 1:
        return tile_grid[..., :band_depth].transpose(0, 1, 3, 2, 4)
    if facing == 2:
        return tile_grid[:, :, ::-1][:, :, :band_depth].transpose(0, 1, 3, 4, 2)
    return tile_grid[:, :, :band_depth].transpose(0, 1, 3, 4, 2)


def place_edge(band_part, facing, points):
    band_depth = band_part.shape[4]
    if facing < 2:
        widened = jnp.pad(
            band_part.transpose(0, 1, 3, 2, 4),
            ((0, 0), (0, 0), (0, 0), (0, 0), (0, points - band_depth)),
        )
        if facing == 0:
            return widened[..., ::-1]
        return widened
    widened = jnp.pad(
        band_part.transpose(0, 1, 4, 2, 3),
        ((0, 0), (0, 0), (0, points - band_depth), (0, 0), (0, 0)),
    )
    if facing == 2:
        return widened[:, :, ::-1]
    return widened


def make_tables(along_cell, across, frac_pair):
    weight_along = (frac_pair[0].astype(jnp.float32) + 0.5) / 256.0
    weight_across = (frac_pair[1].astype(jnp.float32) + 0.5) / 256.0
    return (along_cell, across, weight_along, weight_across)


def weight_tables(tables, points, band_depth):
    along_cell, across, weight_along, weight_across = tables
    along_iota = jnp.arange(points, dtype=jnp.int32)[None, None, :, None]
    across_iota = jnp.arange(band_depth, dtype=jnp.int32)[None, None, :, None]
    cell_now = along_cell[:, :, None, :]
    depth_now = across[:, :, None, :]
    frac_along = weight_along[:, :, None, :]
    frac_across = weight_across[:, :, None, :]
    along_table = (1.0 - frac_along) * (along_iota == cell_now).astype(jnp.float32) + frac_along * (
        along_iota == cell_now + 1
    ).astype(jnp.float32)
    across_table = (1.0 - frac_across) * (across_iota == depth_now).astype(
        jnp.float32
    ) + frac_across * (across_iota == depth_now + 1).astype(jnp.float32)
    return (along_table, across_table)


def interpolate(band_part, tables):
    along_table, across_table = weight_tables(tables, band_part.shape[3], band_part.shape[4])
    partial_sum = jnp.einsum(
        "cabiq,abis->cabqs", band_part, along_table, precision=lax.Precision.HIGHEST
    )
    return jnp.sum(partial_sum * across_table[None], axis=3)


def spread_back(residual, tables, points, band_depth):
    along_table, across_table = weight_tables(tables, points, band_depth)
    weighted = residual[:, :, :, None, :] * across_table[None]
    return jnp.einsum("cabqs,abis->cabiq", weighted, along_table, precision=lax.Precision.HIGHEST)


def bending(control, tile_rows, tile_cols):
    grid_view = tile_view(control, tile_rows, tile_cols, GRID)
    inner = (
        grid_view[:, :, :-2, :, 1:-1]
        + grid_view[:, :, 2:, :, 1:-1]
        + grid_view[:, :, 1:-1, :, :-2]
        + grid_view[:, :, 1:-1, :, 2:]
        - 4.0 * grid_view[:, :, 1:-1, :, 1:-1]
    )
    widths = ((0, 0), (0, 0), (1, 1), (0, 0), (1, 1))
    curvature = jnp.pad(inner, widths)
    padded = jnp.pad(curvature, widths)
    result = (
        padded[:, :, :-2, :, 1:-1]
        + padded[:, :, 2:, :, 1:-1]
        + padded[:, :, 1:-1, :, :-2]
        + padded[:, :, 1:-1, :, 2:]
        - 4.0 * curvature
    )
    return result.reshape(control.shape)


def _halo_kernel(names, send_ref, recv_ref, send_sems, recv_sems):
    ncol = lax.axis_size("col")
    nrow = lax.axis_size("row")
    ci = lax.axis_index("col")
    ri = lax.axis_index("row")

    def dev(c, r):
        where = {"col": c, "row": r}
        return tuple(where[n] for n in names)

    peers = [
        dev((ci + 1) % ncol, ri),
        dev((ci + ncol - 1) % ncol, ri),
        dev(ci, (ri + 1) % nrow),
        dev(ci, (ri + nrow - 1) % nrow),
    ]
    barrier = pltpu.get_barrier_semaphore()
    for peer in peers:
        pl.semaphore_signal(barrier, 1, device_id=peer, device_id_type=MESH_ID)
    pl.semaphore_wait(barrier, len(peers))
    copies = [
        pltpu.make_async_remote_copy(
            src_ref=send_ref.at[k], dst_ref=recv_ref.at[k], send_sem=send_sems.at[k],
            recv_sem=recv_sems.at[k], device_id=peers[k], device_id_type=MESH_ID)
        for k in range(4)
    ]
    for copy in copies:
        copy.start()
    for copy in copies:
        copy.wait_send()
        copy.wait_recv()


def halo_exchange(names, to_east, to_west, to_south, to_north):
    slabs = [to_east, to_west, to_south, to_north]
    rows = max(slab.shape[0] for slab in slabs)
    lanes = slabs[0].shape[1]
    stacked = jnp.stack([jnp.pad(slab, ((0, rows - slab.shape[0]), (0, 0))) for slab in slabs])
    got = pl.pallas_call(
        functools.partial(_halo_kernel, names),
        out_shape=jax.ShapeDtypeStruct(stacked.shape, jnp.float32),
        in_specs=[pl.BlockSpec(memory_space=pltpu.VMEM)],
        out_specs=pl.BlockSpec(memory_space=pltpu.VMEM),
        scratch_shapes=[pltpu.SemaphoreType.DMA((4,)), pltpu.SemaphoreType.DMA((4,))],
        compiler_params=pltpu.CompilerParams(collective_id=1, has_side_effects=True),
    )(stacked)
    return [got[k, : slabs[k].shape[0]] for k in range(4)]


def all_weight_tables(tables):
    pairs = [weight_tables(tables[facing], GRID, BAND) for facing in range(4)]
    return (jnp.stack([pair[0] for pair in pairs]), jnp.stack([pair[1] for pair in pairs]))


def seam_term(control, target, tables, adjacency, names):
    tile_rows, tile_cols = (adjacency.shape[1], adjacency.shape[2])
    along_table, across_table = tables
    grid_view = tile_view(control, tile_rows, tile_cols, GRID)
    bands = jnp.stack([edge_band(grid_view, facing, BAND) for facing in range(4)])
    partial_sum = jnp.einsum(
        "kcabiq,kabis->kcabqs", bands, along_table, precision=lax.Precision.HIGHEST
    )
    stacked_values = jnp.sum(partial_sum * across_table[:, None], axis=4)
    seam_values = [stacked_values[facing] for facing in range(4)]
    samples = seam_values[0].shape[3]
    col_pos = lax.axis_index("col") * tile_cols + jnp.arange(tile_cols)
    row_pos = lax.axis_index("row") * tile_rows + jnp.arange(tile_rows)
    mask_east = (
        adjacency[0].astype(jnp.float32)
        * (col_pos < lax.axis_size("col") * tile_cols - 1).astype(jnp.float32)[None, :]
    )
    mask_south = (
        adjacency[1].astype(jnp.float32)
        * (row_pos < lax.axis_size("row") * tile_rows - 1).astype(jnp.float32)[:, None]
    )
    own_east = seam_values[0]
    own_south = seam_values[2]
    if target is not None:
        own_east = own_east - target[0]
        own_south = own_south - target[1]
    to_east = jnp.concatenate(
        [
            own_east[:, :, -1].reshape(2 * tile_rows, samples),
            jnp.broadcast_to(mask_east[:, -1:], (tile_rows, samples)),
        ]
    )
    to_west = seam_values[1][:, :, 0].reshape(2 * tile_rows, samples)
    to_south = jnp.concatenate(
        [
            own_south[:, -1].reshape(2 * tile_cols, samples),
            jnp.broadcast_to(mask_south[-1][:, None], (tile_cols, samples)),
        ]
    )
    to_north = seam_values[3][:, 0].reshape(2 * tile_cols, samples)
    got_west, got_east, got_north, got_south = halo_exchange(
        names, to_east, to_west, to_south, to_north
    )
    west_east = got_west[: 2 * tile_rows].reshape(2, tile_rows, 1, samples)
    west_mask = got_west[2 * tile_rows :].reshape(1, tile_rows, 1, samples)
    east_next = got_east.reshape(2, tile_rows, 1, samples)
    north_south = got_north[: 2 * tile_cols].reshape(2, 1, tile_cols, samples)
    north_mask = got_north[2 * tile_cols :].reshape(1, 1, tile_cols, samples)
    south_next = got_south.reshape(2, 1, tile_cols, samples)
    west_next = jnp.concatenate([seam_values[1][:, :, 1:], east_next], axis=2)
    north_next = jnp.concatenate([seam_values[3][:, 1:], south_next], axis=1)
    resid_east = (own_east - west_next) * mask_east[None, :, :, None]
    resid_south = (own_south - north_next) * mask_south[None, :, :, None]
    from_west = (west_east - seam_values[1][:, :, :1]) * west_mask
    from_north = (north_south - seam_values[3][:, :1]) * north_mask
    resid_west = -jnp.concatenate([from_west, resid_east[:, :, :-1]], axis=2)
    resid_north = -jnp.concatenate([from_north, resid_south[:, :-1]], axis=1)
    residuals = jnp.stack([resid_east, resid_west, resid_south, resid_north])
    weighted = residuals[:, :, :, :, None, :] * across_table[:, None]
    spread_parts = jnp.einsum(
        "kcabqs,kabis->kcabiq", weighted, along_table, precision=lax.Precision.HIGHEST
    )
    summed = (
        place_edge(spread_parts[0], 0, GRID)
        + place_edge(spread_parts[1], 1, GRID)
        + place_edge(spread_parts[2], 2, GRID)
        + place_edge(spread_parts[3], 3, GRID)
    )
    return summed.reshape(control.shape)


def hessian_apply(control, tables, adjacency, names):
    tile_rows, tile_cols = (adjacency.shape[1], adjacency.shape[2])
    return (
        seam_term(control, None, tables, adjacency, names)
        + BEND_WEIGHT * bending(control, tile_rows, tile_cols)
        + DAMPING * control
    )


def shards(names, start_field, seam_target, seam_rows, seam_band, seam_frac, adjacency):
    tile_rows, tile_cols = (adjacency.shape[1], adjacency.shape[2])
    samples = seam_rows.shape[2] // tile_cols
    along_cells = seam_rows.reshape(4, tile_rows, tile_cols, samples)
    across_cells = seam_band.reshape(4, tile_rows, tile_cols, samples)
    frac_cells = seam_frac.reshape(4, 2, tile_rows, tile_cols, samples)
    tables = [
        make_tables(along_cells[facing], across_cells[facing], frac_cells[facing])
        for facing in range(4)
    ]
    tables = all_weight_tables(tables)
    target_cells = seam_target.reshape(2, 2, tile_rows, tile_cols, samples)
    target = (target_cells[0], target_cells[1])
    control = start_field
    gradient = seam_term(control, target, tables, adjacency, names) + BEND_WEIGHT * bending(
        control, tile_rows, tile_cols
    )
    residual = -gradient
    update = jnp.zeros_like(control)
    direction = residual
    norm_tile = jnp.zeros((8, 128), jnp.float32)
    for iteration in range(ITERS):
        hess_image = hessian_apply(direction, tables, adjacency, names)
        update, residual, direction, norm_tile = cg_step(
            names, iteration, direction, hess_image, residual, update, norm_tile
        )
    control = control + update
    return (control, residual)


def solution(mesh):
    placed = (
        P(None, "row", "col"),
        P(None, None, "row", "col"),
        P(None, "row", "col"),
        P(None, "row", "col"),
        P(None, None, "row", "col"),
        P(None, "row", "col"),
    )
    return jax.shard_map(
        functools.partial(shards, tuple(mesh.axis_names)),
        mesh=mesh,
        in_specs=placed,
        out_specs=(P(None, "row", "col"), P(None, "row", "col")),
        check_vma=False,
    )
```

profile of v0, /device:TPU:1, one launch (start us, length us, event | category | flops | bytes accessed | tf_op | source)
XLA Modules:
  0.0 171.2 jit_solution(15068275310139185379)
XLA Ops:
  0.6 1.1 reshape.881
  6.9 1.7 %fusion.7 = f32[4,2,2,8,256]{4,1,3,2,0:T(2,128)S(1)} fusion(f32[1,2,2,8,32,4]{4,5,1,3,2,0:T(4,128)S(1)} %bitcast.585, f32[1,2,2,8,32,4]{4,5,1,3,2,0:T(4,128)S(1)} %bitcast.586, f32[1,2,2,8,32,4]{4,5,1,3,2,0:T(4,128)S(1)} %bitcast.573, f32[1,2,2,8,32,4]{4,5,1,3,2,0:T(4,128)S(1)} %bitcast.587, f32[4,2,8,4,256]{4,3,2,1,0:T(4,128)S(1)} %pad_maximum_fusion, ...), kind=kOutput, calls=%fused_computation.12 | convolution fusion | flops 52183040 | bytes 2555904 | tf_op jit(solution)/shard_map/kcabiq,kabis->kcabqs/dot_general | solution.py:310
  10.6 0.7 pad_maximum_fusion.5.send_ref
  11.2 11.5 %shard_map.77 = f32[4,24,256]{2,1,0:T(8,128)} custom-call(f32[4,24,256]{2,1,0:T(8,128)} %pad_maximum_fusion.5.send_ref), custom_call_target="tpu_custom_call" | custom-call | tf_op jit(solution)/shard_map/pallas_call | solution.py:289
  22.8 0.7 slice_bitcast_fusion.27
  23.5 0.7 slice_bitcast_fusion.31
  24.2 0.7 slice_bitcast_fusion.39
  25.0 0.7 fusion.138
  26.0 0.7 slice_bitcast_fusion.35
  27.0 2.0 %convolution_bitcast_fusion.7 = f32[4,2,2,8,32,4]{4,5,1,3,2,0:T(4,128)S(1)} fusion(f32[4,2,2,8,256]{4,1,3,2,0:T(2,128)S(1)} %copy.574, f32[4,2,8,4,256]{4,3,2,1,0:T(4,128)S(1)} %pad_maximum_fusion, f32[1,2,8,32,256]{4,3,2,1,0:T(8,128)S(1)} %get-tuple-element.150, f32[1,2,8,32,256]{4,3,2,1,0:T(8,128)S(1)} %get-tuple-element.151, ...), kind=kOutput, calls=%fused_computation.16 | convolution fusion | flops 52035584 | bytes 2555904 | tf_op jit(solution)/shard_map/kcabqs,kabis->kcabiq/dot_general | solution.py:364
  33.5 2.8 %fusion.6 = f32[4,2,2,8,256]{4,1,3,2,0:T(2,128)S(1)} fusion(f32[1,2,2,8,32,4]{4,5,1,3,2,0:T(4,128)S(1)} %get-tuple-element.43, f32[1,2,2,8,32,4]{4,5,1,3,2,0:T(4,128)S(1)} %bitcast.590, f32[1,2,2,8,32,4]{4,5,1,3,2,0:T(4,128)S(1)} %bitcast.574, f32[1,2,2,8,32,4]{4,5,1,3,2,0:T(4,128)S(1)} %bitcast.593, f32[4,2,8,4,256]{4,3,2,1,0:T(4,128)} %copy-done.15, ...), kind=kOutput, calls=%fused_computation.11 | convolution fusion | flops 52183040 | bytes 2555904 | tf_op jit(solution)/shard_map/kcabiq,kabis->kcabqs/dot_general | solution.py:310
  37.3 8.5 %shard_map.78 = f32[4,24,256]{2,1,0:T(8,128)} custom-call(f32[4,24,256]{2,1,0:T(8,128)} %pad_maximum_fusion.6.send_ref), custom_call_target="tpu_custom_call" | custom-call | tf_op jit(solution)/shard_map/pallas_call | solution.py:289
  45.8 0.7 slice_bitcast_fusion.25
  46.5 0.7 slice_bitcast_fusion.30
  47.4 0.7 fusion.137
  48.5 0.7 slice_bitcast_fusion.34
  49.3 2.0 %convolution_bitcast_fusion.6 = f32[4,2,2,8,32,4]{4,5,1,3,2,0:T(4,128)S(1)} fusion(f32[4,2,8,4,256]{4,3,2,1,0:T(4,128)S(1)} %copy-done.16, f32[1,2,8,32,256]{4,3,2,1,0:T(8,128)S(1)} %get-tuple-element.150, f32[1,2,8,32,256]{4,3,2,1,0:T(8,128)S(1)} %copy-done.5, f32[1,2,8,32,256]{4,3,2,1,0:T(8,128)S(1)} %copy-done.8, ...), kind=kOutput, calls=%fused_computation.15 | convolution fusion | flops 52035584 | bytes 2555904 | tf_op jit(solution)/shard_map/kcabqs,kabis->kcabiq/dot_general | solution.py:364
  53.2 0.7 multiply_add_fusion.2.h_ref
  53.9 0.7 reshape.886.u_ref
  55.2 22.8 %shard_map.79 = (f32[128,256]{1,0:T(8,128)}, f32[128,256]{1,0:T(8,128)}, f32[128,256]{1,0:T(8,128)}, f32[8,128]{1,0:T(8,128)}) custom-call(f32[128,256]{1,0:T(8,128)} %copy-done, f32[128,256]{1,0:T(8,128)} %multiply_add_fusion.2.h_ref, f32[128,256]{1,0:T(8,128)} %copy-done, f32[128,256]{1,0:T(8,128)} %reshape.886.u_ref, f32[8,128]{1,0:T(8,128)} %broadcast_in_dim.14.rr_ref), custom_call_target="tpu_custom_call" | custom-call | tf_op jit(solution)/shard_map/pallas_call | solution.py:133
  78.0 1.1 reshape_reshape.8
  80.3 0.7 slice.704
  82.5 2.7 %fusion.5 = f32[4,2,2,8,256]{4,1,3,2,0:T(2,128)S(1)} fusion(f32[1,2,2,8,32,4]{4,5,1,3,2,0:T(4,128)S(1)} %bitcast.588, f32[1,2,2,8,32,4]{4,5,1,3,2,0:T(4,128)S(1)} %bitcast.591, f32[1,2,2,8,32,4]{4,5,1,3,2,0:T(4,128)S(1)} %bitcast.575, f32[1,2,2,8,32,4]{4,5,1,3,2,0:T(4,128)S(1)} %bitcast.594, f32[4,2,8,4,256]{4,3,2,1,0:T(4,128)S(1)} %copy-done.16, ...), kind=kOutput, calls=%fused_computation.10 | convolution fusion | flops 52183040 | bytes 2555904 | tf_op jit(solution)/shard_map/kcabiq,kabis->kcabqs/dot_general | solution.py:310
  86.5 6.4 %shard_map.80 = f32[4,24,256]{2,1,0:T(8,128)} custom-call(f32[4,24,256]{2,1,0:T(8,128)} %pad_maximum_fusion.7.send_ref), custom_call_target="tpu_custom_call" | custom-call | tf_op jit(solution)/shard_map/pallas_call | solution.py:289
  92.9 0.7 slice_bitcast_fusion.23
  93.6 0.7 slice_bitcast_fusion.29
  94.3 0.7 slice_bitcast_fusion.38
  95.2 0.7 fusion.136
  96.1 0.7 slice_bitcast_fusion.33
  97.1 2.0 %convolution_bitcast_fusion.5 = f32[4,2,2,8,32,4]{4,5,1,3,2,0:T(4,128)S(1)} fusion(f32[4,2,2,8,256]{4,1,3,2,0:T(2,128)S(1)} %copy.625, f32[4,2,8,4,256]{4,3,2,1,0:T(4,128)S(1)} %copy-done.16, f32[1,2,8,32,256]{4,3,2,1,0:T(8,128)S(1)} %get-tuple-element.150, f32[1,2,8,32,256]{4,3,2,1,0:T(8,128)S(1)} %copy-done.6, f32[1,2,8,32,256]{4,3,2,1,0:T(8,128)S(1)} %copy-done.9, ...), kind=kOutput, calls=%fused_computation.14 | convolution fusion | flops 52035584 | bytes 2555904 | tf_op jit(solution)/shard_map/kcabqs,kabis->kcabiq/dot_general | solution.py:364
  101.0 0.7 copy-done.2
  101.7 0.7 multiply_add_fusion.1.h_ref
  102.4 19.9 %shard_map.81 = (f32[128,256]{1,0:T(8,128)}, f32[128,256]{1,0:T(8,128)}, f32[128,256]{1,0:T(8,128)}, f32[8,128]{1,0:T(8,128)}) custom-call(f32[128,256]{1,0:T(8,128)} %get-tuple-element.12.d_ref, f32[128,256]{1,0:T(8,128)} %multiply_add_fusion.1.h_ref, f32[128,256]{1,0:T(8,128)} %get-tuple-element.13.r_ref, f32[128,256]{1,0:T(8,128)} %get-tuple-element.14.u_ref, ...), custom_call_target="tpu_custom_call" | custom-call | tf_op jit(solution)/shard_map/pallas_call | solution.py:133
  122.3 1.1 reshape_reshape.9
  125.3 0.7 slice.741
  127.6 2.5 %fusion.4 = f32[4,2,2,8,256]{4,1,3,2,0:T(2,128)S(1)} fusion(f32[1,2,2,8,32,4]{4,5,1,3,2,0:T(4,128)} %bitcast.589, f32[1,2,2,8,32,4]{4,5,1,3,2,0:T(4,128)} %bitcast.592, f32[1,2,2,8,32,4]{4,5,1,3,2,0:T(4,128)S(1)} %bitcast.576, f32[1,2,2,8,32,4]{4,5,1,3,2,0:T(4,128)S(1)} %bitcast.595, f32[4,2,8,4,256]{4,3,2,1,0:T(4,128)S(1)} %copy-done.16, ...), kind=kOutput, calls=%fused_computation.9 | convolution fusion | flops 52183040 | bytes 2555904 | tf_op jit(solution)/shard_map/kcabiq,kabis->kcabqs/dot_general | solution.py:310
  131.4 6.4 %shard_map.82 = f32[4,24,256]{2,1,0:T(8,128)} custom-call(f32[4,24,256]{2,1,0:T(8,128)} %pad_maximum_fusion.8.send_ref), custom_call_target="tpu_custom_call" | custom-call | tf_op jit(solution)/shard_map/pallas_call | solution.py:289
  137.8 0.7 slice_bitcast_fusion.21
  138.5 0.7 slice_bitcast_fusion.28
  139.2 0.7 slice_bitcast_fusion.37
  140.1 0.7 fusion.135
  141.0 0.7 slice_bitcast_fusion.32
  142.0 2.0 %convolution_bitcast_fusion.4 = f32[4,2,2,8,32,4]{4,5,1,3,2,0:T(4,128)S(1)} fusion(f32[4,2,2,8,256]{4,1,3,2,0:T(2,128)S(1)} %copy.651, f32[4,2,8,4,256]{4,3,2,1,0:T(4,128)S(1)} %copy-done.16, f32[1,2,8,32,256]{4,3,2,1,0:T(8,128)S(1)} %get-tuple-element.150, f32[1,2,8,32,256]{4,3,2,1,0:T(8,128)S(1)} %copy-done.6, f32[1,2,8,32,256]{4,3,2,1,0:T(8,128)S(1)} %copy-done.10, ...), kind=kOutput, calls=%fused_computation.13 | convolution fusion | flops 52035584 | bytes 2555904 | tf_op jit(solution)/shard_map/kcabqs,kabis->kcabiq/dot_general | solution.py:364
  145.8 0.7 copy-done.1
  146.6 0.7 multiply_add_fusion.h_ref
  147.2 20.8 %shard_map.83 = (f32[128,256]{1,0:T(8,128)}, f32[128,256]{1,0:T(8,128)}) custom-call(f32[128,256]{1,0:T(8,128)} %get-tuple-element.16.d_ref, f32[128,256]{1,0:T(8,128)} %multiply_add_fusion.h_ref, f32[128,256]{1,0:T(8,128)} %get-tuple-element.17.r_ref, f32[128,256]{1,0:T(8,128)} %get-tuple-element.18.u_ref, f32[8,128]{1,0:T(8,128)} %get-tuple-element.19.rr_ref), custom_call_target="tpu_custom_call" | custom-call | tf_op jit(solution)/shard_map/pallas_call | solution.py:133
  168.0 1.6 add.561
  169.6 1.6 copy.938
  (336 shorter events, 28.8 us)
Async XLA Ops:
  2.7 0.8 copy-start.18
  3.9 0.9 copy-start.17
  4.2 0.9 copy-start.19
  5.3 0.8 copy-start.20
  5.5 21.5 %copy-start.15 = (f32[4,2,8,4,256]{4,3,2,1,0:T(4,128)}, f32[4,2,8,4,256]{4,3,2,1,0:T(4,128)S(1)}, u32[]{:S(2)}) copy-start(f32[4,2,8,4,256]{4,3,2,1,0:T(4,128)S(1)} %pad_maximum_fusion) | copy-start | bytes 786436
  6.5 20.5 %copy-start.4 = (f32[1,2,8,32,256]{4,3,2,1,0:T(8,128)}, f32[1,2,8,32,256]{4,3,2,1,0:T(8,128)S(1)}, u32[]{:S(2)}) copy-start(f32[1,2,8,32,256]{4,3,2,1,0:T(8,128)S(1)} %get-tuple-element.151) | copy-start | bytes 1572868
  6.9 20.1 %copy-start.7 = (f32[1,2,8,32,256]{4,3,2,1,0:T(8,128)}, f32[1,2,8,32,256]{4,3,2,1,0:T(8,128)S(1)}, u32[]{:S(2)}) copy-start(f32[1,2,8,32,256]{4,3,2,1,0:T(8,128)S(1)} %get-tuple-element.152) | copy-start | bytes 1572868
  6.9 20.1 %copy-start.11 = (f32[1,2,8,32,256]{4,3,2,1,0:T(8,128)}, f32[1,2,8,32,256]{4,3,2,1,0:T(8,128)S(1)}, u32[]{:S(2)}) copy-start(f32[1,2,8,32,256]{4,3,2,1,0:T(8,128)S(1)} %get-tuple-element.153) | copy-start | bytes 1572868
  8.7 0.7 copy-start.29
  9.5 0.5 copy-start.25
  10.5 26.1 %copy-start.22 = (f32[6]{0:T(128)}, f32[6]{0:T(128)S(1)}, u32[]{:S(2)}) copy-start(f32[6]{0:T(128)S(1)} %pad.258.clone) | copy-start | bytes 76
  30.9 22.3 %copy-start = (f32[128,256]{1,0:T(8,128)}, f32[128,256]{1,0:T(8,128)S(1)}, u32[]{:S(2)}) copy-start(f32[128,256]{1,0:T(8,128)S(1)} %neg.92.d_ref.r_ref) | copy-start | bytes 393220
  31.9 1.0 copy-start.12
  32.1 1.1 copy-start.5
  32.4 1.1 copy-start.8
  33.5 2.9 %copy-start.26 = (f32[24]{0:T(128)S(1)}, f32[24]{0:T(128)}, u32[]{:S(2)}) copy-start(f32[24]{0:T(128)} %copy-done.25) | copy-start | bytes 292
  47.2 2.1 %copy-start.16 = (f32[4,2,8,4,256]{4,3,2,1,0:T(4,128)S(1)}, f32[4,2,8,4,256]{4,3,2,1,0:T(4,128)}, u32[]{:S(2)}) copy-start(f32[4,2,8,4,256]{4,3,2,1,0:T(4,128)} %copy-done.15) | copy-start | bytes 786436
  81.2 1.0 copy-start.6
  81.2 1.2 copy-start.9
  81.5 0.9 copy-start.21
  82.5 2.8 %copy-start.27 = (f32[24]{0:T(128)S(1)}, f32[24]{0:T(128)}, u32[]{:S(2)}) copy-start(f32[24]{0:T(128)} %copy-done.25) | copy-start | bytes 292
  85.2 0.6 copy-start.23
  95.9 1.1 copy-start.13
  100.8 0.9 copy-start.2
  126.2 1.0 copy-start.10
  126.5 1.1 copy-start.14
  127.6 2.6 %copy-start.28 = (f32[24]{0:T(128)S(1)}, f32[24]{0:T(128)}, u32[]{:S(2)}) copy-start(f32[24]{0:T(128)} %copy-done.25) | copy-start | bytes 292
  130.1 0.6 copy-start.24
  145.7 0.9 copy-start.1
  146.6 21.5 %copy-start.3 = (f32[2,64,256]{2,1,0:T(8,128)S(1)}, f32[2,64,256]{2,1,0:T(8,128)}, u32[]{:S(2)}) copy-start(f32[2,64,256]{2,1,0:T(8,128)} %param.6) | copy-start | bytes 393220
where the time goes:
time: 173 us; the launch traced here: 171 us
  Pallas kernels  96.3 us (56%)
  local copies, waits for them, and re-layouts  39.7 us (23%)
  matrix products  17.8 us (10%)
  other arithmetic  15.1 us (9%)
  between operations  2.22 us (1%)
    pallas_call x3, Pallas kernels, cg_step(): pl.pallas_call(functools.partial(_cg_kernel, names, first, last), out_sha...  63.5 us
    pallas_call x4, Pallas kernels, halo_exchange(): pl.pallas_call(functools.partial(_halo_kernel, names), out_shape=jax.Shap...  32.8 us
    unnamed x109, local copies, waits for them, and re-layouts  13.6 us
    dot_general x4, matrix products, seam_term(): jnp.einsum('kcabiq,kabis->kcabqs', bands, along_table, precision=lax.Prec...  9.83 us
    dot_general x4, matrix products, seam_term(): jnp.einsum('kcabqs,kabis->kcabiq', weighted, along_table, precision=lax.P...  7.95 us

commit v1 on v0

--- a/solution.py
+++ b/solution.py
@@ -34,9 +34,34 @@
         where = {"col": c, "row": r}
         return tuple(where[n] for n in names)
 
+    barrier = pltpu.get_barrier_semaphore()
+
+    @pl.loop(1, nrow)
+    def _(k):
+        pl.semaphore_signal(barrier, 1, device_id=dev(ci, (ri + k) % nrow), device_id_type=MESH_ID)
+
+    @pl.loop(1, ncol)
+    def _(k):
+        pl.semaphore_signal(barrier, 1, device_id=dev((ci + k) % ncol, ri), device_id_type=MESH_ID)
+
     direction = d_ref[...]
-    image = h_ref[...]
     residual = r_ref[...]
+    rows, cols = direction.shape
+    y = lax.broadcasted_iota(jnp.int32, (rows, cols), 0) % GRID
+    x = lax.broadcasted_iota(jnp.int32, (rows, cols), 1) % GRID
+    inside = (y >= 1) & (y <= GRID - 2) & (x >= 1) & (x <= GRID - 2)
+
+    def five_point(f):
+        return (
+            pltpu.roll(f, 1, 0)
+            + pltpu.roll(f, rows - 1, 0)
+            + pltpu.roll(f, 1, 1)
+            + pltpu.roll(f, cols - 1, 1)
+            - 4.0 * f
+        )
+
+    curvature = jnp.where(inside, five_point(direction), 0.0)
+    image = h_ref[...] + BEND_WEIGHT * five_point(curvature) + DAMPING * direction
 
     def total(x):
         return jnp.sum(jnp.sum(x, axis=0, keepdims=True), axis=1, keepdims=True)
@@ -52,16 +77,6 @@
     for k, value in enumerate(parts):
         tile = jnp.where((sub == 0) & (lane == k), value, tile)
     mine[...] = tile
-
-    barrier = pltpu.get_barrier_semaphore()
-
-    @pl.loop(1, nrow)
-    def _(k):
-        pl.semaphore_signal(barrier, 1, device_id=dev(ci, (ri + k) % nrow), device_id_type=MESH_ID)
-
-    @pl.loop(1, ncol)
-    def _(k):
-        pl.semaphore_signal(barrier, 1, device_id=dev((ci + k) % ncol, ri), device_id_type=MESH_ID)
 
     pl.semaphore_wait(barrier, nrow - 1 + ncol - 1)
 
@@ -404,9 +419,9 @@
     direction = residual
     norm_tile = jnp.zeros((8, 128), jnp.float32)
     for iteration in range(ITERS):
-        hess_image = hessian_apply(direction, tables, adjacency, names)
+        seam_image = seam_term(direction, None, tables, adjacency, names)
         update, residual, direction, norm_tile = cg_step(
-            names, iteration, direction, hess_image, residual, update, norm_tile
+            names, iteration, direction, seam_image, residual, update, norm_tile
         )
     control = control + update
     return (control, residual)

time: 173 us -> 166 us (0.960)
  other arithmetic: 15.1 us -> 10.9 us
  matrix products: 17.8 us -> 15.9 us
    add x6 -> x3, other arithmetic: 3.26 us -> 0.5 us  [seam_term(): place_edge(spread_parts[0], 0, GRID) + place_edge(spread_parts[1], 1, GRID)]
    another operation x0 -> x3, local copies, waits for them, and re-layouts: none -> 2.52 us  [cg_step(): fields = [x.reshape(flat) for x in (direction, image, residual, update)]]
    unnamed x109 -> x99, local copies, waits for them, and re-layouts: 13.6 us -> 11.4 us
    dot_general x4, matrix products: 9.83 us -> 7.92 us  [seam_term(): jnp.einsum('kcabiq,kabis->kcabqs', bands, along_table, precision=lax.Prec...]
where the time goes in v1:
time: 166 us; the launch traced here: 164 us
  Pallas kernels  95.5 us (58%)
  local copies, waits for them, and re-layouts  39.6 us (24%)
  matrix products  15.9 us (10%)
  other arithmetic  10.9 us (7%)
  between operations  2.16 us (1%)
    pallas_call x3, Pallas kernels, cg_step(): pl.pallas_call(functools.partial(_cg_kernel, names, first, last), out_sha...  62.7 us
    pallas_call x4, Pallas kernels, halo_exchange(): pl.pallas_call(functools.partial(_halo_kernel, names), out_shape=jax.Shap...  32.8 us
    unnamed x99, local copies, waits for them, and re-layouts  11.4 us
    dot_general x4, matrix products, seam_term(): jnp.einsum('kcabqs,kabis->kcabiq', weighted, along_table, precision=lax.P...  7.94 us
    dot_general x4, matrix products, seam_term(): jnp.einsum('kcabiq,kabis->kcabqs', bands, along_table, precision=lax.Prec...  7.92 us

profile of v1, /device:TPU:1, one launch (start us, length us, event | category | flops | bytes accessed | tf_op | source)
XLA Modules:
  0.0 164.1 jit_solution(2084421634330224736)
XLA Ops:
  0.6 1.1 reshape.852
  3.6 0.7 slice.535
  5.1 0.7 slice.532
  8.5 1.7 %fusion.7 = f32[4,2,2,8,256]{4,1,3,2,0:T(2,128)S(1)} fusion(f32[1,2,2,8,32,4]{4,5,1,3,2,0:T(4,128)S(1)} %bitcast.585, f32[1,2,2,8,32,4]{4,5,1,3,2,0:T(4,128)S(1)} %bitcast.586, f32[1,2,2,8,32,4]{4,5,1,3,2,0:T(4,128)S(1)} %bitcast.573, f32[1,2,2,8,32,4]{4,5,1,3,2,0:T(4,128)S(1)} %bitcast.587, f32[4,2,8,4,256]{4,3,2,1,0:T(4,128)S(1)} %pad_maximum_fusion, ...), kind=kOutput, calls=%fused_computation.12 | convolution fusion | flops 52183040 | bytes 2555904 | tf_op jit(solution)/shard_map/kcabiq,kabis->kcabqs/dot_general | solution.py:325
  12.7 11.6 %shard_map.77 = f32[4,24,256]{2,1,0:T(8,128)} custom-call(f32[4,24,256]{2,1,0:T(8,128)} %pad_maximum_fusion.5.send_ref), custom_call_target="tpu_custom_call" | custom-call | tf_op jit(solution)/shard_map/pallas_call | solution.py:304
  24.2 0.7 slice_bitcast_fusion.27
  24.9 0.7 slice_bitcast_fusion.31
  25.6 0.7 slice_bitcast_fusion.39
  26.5 0.7 fusion.115
  27.5 0.7 slice_bitcast_fusion.35
  28.5 2.0 %convolution_bitcast_fusion.7 = f32[4,2,2,8,32,4]{4,5,1,3,2,0:T(4,128)S(1)} fusion(f32[4,2,2,8,256]{4,1,3,2,0:T(2,128)S(1)} %copy.524, f32[4,2,8,4,256]{4,3,2,1,0:T(4,128)S(1)} %pad_maximum_fusion, f32[1,2,8,32,256]{4,3,2,1,0:T(8,128)S(1)} %get-tuple-element.140, f32[1,2,8,32,256]{4,3,2,1,0:T(8,128)S(1)} %get-tuple-element.141, ...), kind=kOutput, calls=%fused_computation.16 | convolution fusion | flops 52035584 | bytes 2555904 | tf_op jit(solution)/shard_map/kcabqs,kabis->kcabiq/dot_general | solution.py:379
  32.2 0.8 neg.91.d_ref.r_ref
  34.6 2.7 %fusion.6 = f32[4,2,2,8,256]{4,1,3,2,0:T(2,128)S(1)} fusion(f32[1,2,2,8,32,4]{4,5,1,3,2,0:T(4,128)S(1)} %get-tuple-element.33, f32[1,2,2,8,32,4]{4,5,1,3,2,0:T(4,128)S(1)} %bitcast.590, f32[1,2,2,8,32,4]{4,5,1,3,2,0:T(4,128)S(1)} %bitcast.574, f32[1,2,2,8,32,4]{4,5,1,3,2,0:T(4,128)S(1)} %bitcast.593, f32[4,2,8,4,256]{4,3,2,1,0:T(4,128)S(1)} %pad_maximum_fusion, ...), kind=kOutput, calls=%fused_computation.11 | convolution fusion | flops 52183040 | bytes 2555904 | tf_op jit(solution)/shard_map/kcabiq,kabis->kcabqs/dot_general | solution.py:325
  38.3 8.5 %shard_map.78 = f32[4,24,256]{2,1,0:T(8,128)} custom-call(f32[4,24,256]{2,1,0:T(8,128)} %pad_maximum_fusion.6.send_ref), custom_call_target="tpu_custom_call" | custom-call | tf_op jit(solution)/shard_map/pallas_call | solution.py:304
  46.7 0.7 slice_bitcast_fusion.25
  47.5 0.7 slice_bitcast_fusion.30
  48.3 0.8 fusion.114
  49.5 0.7 slice_bitcast_fusion.34
  50.3 2.0 %convolution_bitcast_fusion.6 = f32[4,2,2,8,32,4]{4,5,1,3,2,0:T(4,128)S(1)} fusion(f32[4,2,8,4,256]{4,3,2,1,0:T(4,128)S(1)} %pad_maximum_fusion, f32[1,2,8,32,256]{4,3,2,1,0:T(8,128)S(1)} %get-tuple-element.140, f32[1,2,8,32,256]{4,3,2,1,0:T(8,128)S(1)} %copy-done.2, f32[1,2,8,32,256]{4,3,2,1,0:T(8,128)S(1)} %copy-done.4, ...), kind=kOutput, calls=%fused_computation.15 | convolution fusion | flops 52035584 | bytes 2555904 | tf_op jit(solution)/shard_map/kcabqs,kabis->kcabiq/dot_general | solution.py:379
  53.8 0.8 reshape_reshape.15.h_ref
  54.6 0.7 reshape.857.u_ref
  55.9 22.5 %shard_map.79 = (f32[128,256]{1,0:T(8,128)}, f32[128,256]{1,0:T(8,128)}, f32[128,256]{1,0:T(8,128)}, f32[8,128]{1,0:T(8,128)}) custom-call(f32[128,256]{1,0:T(8,128)} %neg.91.d_ref.r_ref, f32[128,256]{1,0:T(8,128)} %reshape_reshape.15.h_ref, f32[128,256]{1,0:T(8,128)} %neg.91.d_ref.r_ref, f32[128,256]{1,0:T(8,128)} %reshape.857.u_ref, ...), custom_call_target="tpu_custom_call" | custom-call | tf_op jit(solution)/shard_map/pallas_call | solution.py:148
  78.4 1.1 reshape_reshape.16
  79.6 0.7 slice.614
  81.6 1.7 %fusion.5 = f32[4,2,2,8,256]{4,1,3,2,0:T(2,128)S(1)} fusion(f32[1,2,2,8,32,4]{4,5,1,3,2,0:T(4,128)S(1)} %bitcast.588, f32[1,2,2,8,32,4]{4,5,1,3,2,0:T(4,128)S(1)} %bitcast.591, f32[1,2,2,8,32,4]{4,5,1,3,2,0:T(4,128)S(1)} %bitcast.575, f32[1,2,2,8,32,4]{4,5,1,3,2,0:T(4,128)S(1)} %bitcast.594, f32[4,2,8,4,256]{4,3,2,1,0:T(4,128)S(1)} %pad_maximum_fusion, ...), kind=kOutput, calls=%fused_computation.10 | convolution fusion | flops 52183040 | bytes 2555904 | tf_op jit(solution)/shard_map/kcabiq,kabis->kcabqs/dot_general | solution.py:325
  84.8 6.4 %shard_map.80 = f32[4,24,256]{2,1,0:T(8,128)} custom-call(f32[4,24,256]{2,1,0:T(8,128)} %pad_maximum_fusion.7.send_ref), custom_call_target="tpu_custom_call" | custom-call | tf_op jit(solution)/shard_map/pallas_call | solution.py:304
  91.2 0.7 slice_bitcast_fusion.23
  91.9 0.7 slice_bitcast_fusion.29
  92.6 0.7 slice_bitcast_fusion.38
  93.5 0.7 fusion.113
  94.4 0.7 slice_bitcast_fusion.33
  95.3 2.0 %convolution_bitcast_fusion.5 = f32[4,2,2,8,32,4]{4,5,1,3,2,0:T(4,128)S(1)} fusion(f32[4,2,2,8,256]{4,1,3,2,0:T(2,128)S(1)} %copy.575, f32[4,2,8,4,256]{4,3,2,1,0:T(4,128)S(1)} %pad_maximum_fusion, f32[1,2,8,32,256]{4,3,2,1,0:T(8,128)S(1)} %get-tuple-element.140, f32[1,2,8,32,256]{4,3,2,1,0:T(8,128)S(1)} %copy-done.2, ...), kind=kOutput, calls=%fused_computation.14 | convolution fusion | flops 52035584 | bytes 2555904 | tf_op jit(solution)/shard_map/kcabqs,kabis->kcabiq/dot_general | solution.py:379
  98.8 0.8 reshape_reshape.17.h_ref
  99.6 19.4 %shard_map.81 = (f32[128,256]{1,0:T(8,128)}, f32[128,256]{1,0:T(8,128)}, f32[128,256]{1,0:T(8,128)}, f32[8,128]{1,0:T(8,128)}) custom-call(f32[128,256]{1,0:T(8,128)} %get-tuple-element.12.d_ref, f32[128,256]{1,0:T(8,128)} %reshape_reshape.17.h_ref, f32[128,256]{1,0:T(8,128)} %get-tuple-element.13.r_ref, f32[128,256]{1,0:T(8,128)} %get-tuple-element.14.u_ref, ...), custom_call_target="tpu_custom_call" | custom-call | tf_op jit(solution)/shard_map/pallas_call | solution.py:148
  119.0 1.1 reshape_reshape.18
  120.2 0.7 slice.642
  122.2 1.7 %fusion.4 = f32[4,2,2,8,256]{4,1,3,2,0:T(2,128)S(1)} fusion(f32[1,2,2,8,32,4]{4,5,1,3,2,0:T(4,128)S(1)} %bitcast.589, f32[1,2,2,8,32,4]{4,5,1,3,2,0:T(4,128)S(1)} %bitcast.592, f32[1,2,2,8,32,4]{4,5,1,3,2,0:T(4,128)S(1)} %bitcast.576, f32[1,2,2,8,32,4]{4,5,1,3,2,0:T(4,128)S(1)} %bitcast.595, f32[4,2,8,4,256]{4,3,2,1,0:T(4,128)S(1)} %pad_maximum_fusion, ...), kind=kOutput, calls=%fused_computation.9 | convolution fusion | flops 52183040 | bytes 2555904 | tf_op jit(solution)/shard_map/kcabiq,kabis->kcabqs/dot_general | solution.py:325
  125.4 6.4 %shard_map.82 = f32[4,24,256]{2,1,0:T(8,128)} custom-call(f32[4,24,256]{2,1,0:T(8,128)} %pad_maximum_fusion.8.send_ref), custom_call_target="tpu_custom_call" | custom-call | tf_op jit(solution)/shard_map/pallas_call | solution.py:304
  131.8 0.7 slice_bitcast_fusion.21
  132.5 0.7 slice_bitcast_fusion.28
  133.2 0.7 slice_bitcast_fusion.37
  134.1 0.7 fusion.112
  135.0 0.7 slice_bitcast_fusion.32
  135.9 2.0 %convolution_bitcast_fusion.4 = f32[4,2,2,8,32,4]{4,5,1,3,2,0:T(4,128)S(1)} fusion(f32[4,2,2,8,256]{4,1,3,2,0:T(2,128)S(1)} %copy.596, f32[4,2,8,4,256]{4,3,2,1,0:T(4,128)S(1)} %pad_maximum_fusion, f32[1,2,8,32,256]{4,3,2,1,0:T(8,128)S(1)} %get-tuple-element.140, f32[1,2,8,32,256]{4,3,2,1,0:T(8,128)S(1)} %copy-done.2, ...), kind=kOutput, calls=%fused_computation.13 | convolution fusion | flops 52035584 | bytes 2555904 | tf_op jit(solution)/shard_map/kcabqs,kabis->kcabiq/dot_general | solution.py:379
  139.4 0.8 reshape_reshape.19.h_ref
  140.2 20.7 %shard_map.83 = (f32[128,256]{1,0:T(8,128)}, f32[128,256]{1,0:T(8,128)}) custom-call(f32[128,256]{1,0:T(8,128)} %get-tuple-element.16.d_ref, f32[128,256]{1,0:T(8,128)} %reshape_reshape.19.h_ref, f32[128,256]{1,0:T(8,128)} %get-tuple-element.17.r_ref, f32[128,256]{1,0:T(8,128)} %get-tuple-element.18.u_ref, f32[8,128]{1,0:T(8,128)} %get-tuple-element.19.rr_ref), custom_call_target="tpu_custom_call" | custom-call | tf_op jit(solution)/shard_map/pallas_call | solution.py:148
  161.0 1.6 add.434
  162.5 1.6 copy.842
  (315 shorter events, 23.9 us)
Async XLA Ops:
  2.7 0.8 copy-start.10
  4.6 1.3 copy-start.9
  4.9 1.1 copy-start.11
  6.1 0.8 copy-start.12
  7.4 21.1 %copy-start.1 = (f32[1,2,8,32,256]{4,3,2,1,0:T(8,128)}, f32[1,2,8,32,256]{4,3,2,1,0:T(8,128)S(1)}, u32[]{:S(2)}) copy-start(f32[1,2,8,32,256]{4,3,2,1,0:T(8,128)S(1)} %get-tuple-element.141) | copy-start | bytes 1572868
  7.5 0.9 copy-start.13
  7.5 1.0 copy-start.14
  7.8 20.6 %copy-start.3 = (f32[1,2,8,32,256]{4,3,2,1,0:T(8,128)}, f32[1,2,8,32,256]{4,3,2,1,0:T(8,128)S(1)}, u32[]{:S(2)}) copy-start(f32[1,2,8,32,256]{4,3,2,1,0:T(8,128)S(1)} %get-tuple-element.142) | copy-start | bytes 1572868
  7.8 20.6 %copy-start.5 = (f32[1,2,8,32,256]{4,3,2,1,0:T(8,128)}, f32[1,2,8,32,256]{4,3,2,1,0:T(8,128)S(1)}, u32[]{:S(2)}) copy-start(f32[1,2,8,32,256]{4,3,2,1,0:T(8,128)S(1)} %get-tuple-element.143) | copy-start | bytes 1572868
  10.2 0.7 copy-start.24
  11.0 0.5 copy-start.20
  11.9 25.6 %copy-start.17 = (f32[6]{0:T(128)}, f32[6]{0:T(128)S(1)}, u32[]{:S(2)}) copy-start(f32[6]{0:T(128)S(1)} %pad.234.clone) | copy-start | bytes 76
  33.4 1.0 copy-start.2
  33.4 1.2 copy-start.4
  34.6 2.8 %copy-start.21 = (f32[24]{0:T(128)S(1)}, f32[24]{0:T(128)}, u32[]{:S(2)}) copy-start(f32[24]{0:T(128)} %copy-done.20) | copy-start | bytes 292
  48.2 2.1 %copy-start.6 = (f32[1,2,8,32,256]{4,3,2,1,0:T(8,128)S(1)}, f32[1,2,8,32,256]{4,3,2,1,0:T(8,128)}, u32[]{:S(2)}) copy-start(f32[1,2,8,32,256]{4,3,2,1,0:T(8,128)} %copy-done.5) | copy-start | bytes 1572868
  80.5 1.0 copy-start.7
  80.8 0.9 copy-start.15
  81.6 1.8 %copy-start.22 = (f32[24]{0:T(128)S(1)}, f32[24]{0:T(128)}, u32[]{:S(2)}) copy-start(f32[24]{0:T(128)} %copy-done.20) | copy-start | bytes 292
  83.4 0.7 copy-start.18
  121.1 1.0 copy-start.8
  121.4 0.9 copy-start.16
  122.2 1.8 %copy-start.23 = (f32[24]{0:T(128)S(1)}, f32[24]{0:T(128)}, u32[]{:S(2)}) copy-start(f32[24]{0:T(128)} %copy-done.20) | copy-start | bytes 292
  124.0 0.7 copy-start.19
  139.4 21.6 %copy-start = (f32[2,64,256]{2,1,0:T(8,128)S(1)}, f32[2,64,256]{2,1,0:T(8,128)}, u32[]{:S(2)}) copy-start(f32[2,64,256]{2,1,0:T(8,128)} %param.6) | copy-start | bytes 393220

commit v2 on v1

--- a/solution.py
+++ b/solution.py
@@ -19,7 +19,10 @@
 MESH_ID = pl.DeviceIdType.MESH
 
 
-def _cg_kernel(names, first, last, d_ref, h_ref, r_ref, u_ref, rr_ref, *refs):
+def _cg_kernel(names, first, last, d_ref, h_ref, r_ref, *refs):
+    if not first:
+        u_ref, rr_ref = refs[:2]
+        refs = refs[2:]
     if last:
         u_out, r_out, row_buf, col_buf, mine, part, row_send, row_recv, col_send, col_recv = refs
     else:
@@ -122,7 +125,10 @@
     curv = pick(0)
     norm_now = pick(len(parts) - 1) if first else rr_ref[0:1, 0:1]
     step_size = norm_now / curv
-    u_out[...] = u_ref[...] + step_size * direction
+    if first:
+        u_out[...] = step_size * direction
+    else:
+        u_out[...] = u_ref[...] + step_size * direction
     residual = residual - step_size * image
     r_out[...] = residual
     if not last:
@@ -140,7 +146,9 @@
     last = iteration == ITERS - 1
     shape = direction.shape
     flat = (shape[0] * shape[1], shape[2])
-    fields = [x.reshape(flat) for x in (direction, image, residual, update)]
+    fields = [x.reshape(flat) for x in (direction, image, residual)]
+    if not first:
+        fields += [update.reshape(flat), norm_tile]
     field_type = jax.ShapeDtypeStruct(flat, jnp.float32)
     out_shape = [field_type, field_type]
     if not last:
@@ -148,7 +156,7 @@
     got = pl.pallas_call(
         functools.partial(_cg_kernel, names, first, last),
         out_shape=tuple(out_shape),
-        in_specs=[pl.BlockSpec(memory_space=pltpu.VMEM)] * 5,
+        in_specs=[pl.BlockSpec(memory_space=pltpu.VMEM)] * len(fields),
         out_specs=tuple(pl.BlockSpec(memory_space=pltpu.VMEM) for _ in out_shape),
         scratch_shapes=[
             pltpu.VMEM((nrow, 8, 128), jnp.float32),
@@ -163,7 +171,7 @@
         compiler_params=pltpu.CompilerParams(
             collective_id=10 + iteration, has_side_effects=True
         ),
-    )(*fields, norm_tile)
+    )(*fields)
     update = got[0].reshape(shape)
     residual = got[1].reshape(shape)
     if last:
@@ -415,9 +423,9 @@
         control, tile_rows, tile_cols
     )
     residual = -gradient
-    update = jnp.zeros_like(control)
+    update = None
     direction = residual
-    norm_tile = jnp.zeros((8, 128), jnp.float32)
+    norm_tile = None
     for iteration in range(ITERS):
         seam_image = seam_term(direction, None, tables, adjacency, names)
         update, residual, direction, norm_tile = cg_step(

time: 166 us -> 165 us (level)
  no operation moved by 1% of the time
where the time goes in v2:
time: 165 us; the launch traced here: 163 us
  Pallas kernels  95.4 us (58%)
  local copies, waits for them, and re-layouts  38.4 us (23%)
  matrix products  15.9 us (10%)
  other arithmetic  10.9 us (7%)
  between operations  2.16 us (1%)
    pallas_call x3, Pallas kernels, cg_step(): pl.pallas_call(functools.partial(_cg_kernel, names, first, last), out_sha...  62.6 us
    pallas_call x4, Pallas kernels, halo_exchange(): pl.pallas_call(functools.partial(_halo_kernel, names), out_shape=jax.Shap...  32.8 us
    unnamed x99, local copies, waits for them, and re-layouts  11.4 us
    dot_general x4, matrix products, seam_term(): jnp.einsum('kcabqs,kabis->kcabiq', weighted, along_table, precision=lax.P...  7.94 us
    dot_general x4, matrix products, seam_term(): jnp.einsum('kcabiq,kabis->kcabqs', bands, along_table, precision=lax.Prec...  7.92 us

profile of v2, /device:TPU:1, one launch (start us, length us, event | category | flops | bytes accessed | tf_op | source)
XLA Modules:
  0.0 162.8 jit_solution(4461324460644593694)
XLA Ops:
  0.6 1.1 reshape.849
  3.6 0.7 slice.535
  5.1 0.7 slice.532
  8.5 1.7 %fusion.7 = f32[4,2,2,8,256]{4,1,3,2,0:T(2,128)S(1)} fusion(f32[1,2,2,8,32,4]{4,5,1,3,2,0:T(4,128)S(1)} %bitcast.585, f32[1,2,2,8,32,4]{4,5,1,3,2,0:T(4,128)S(1)} %bitcast.586, f32[1,2,2,8,32,4]{4,5,1,3,2,0:T(4,128)S(1)} %bitcast.573, f32[1,2,2,8,32,4]{4,5,1,3,2,0:T(4,128)S(1)} %bitcast.587, f32[4,2,8,4,256]{4,3,2,1,0:T(4,128)S(1)} %pad_maximum_fusion, ...), kind=kOutput, calls=%fused_computation.12 | convolution fusion | flops 52183040 | bytes 2555904 | tf_op jit(solution)/shard_map/kcabiq,kabis->kcabqs/dot_general | solution.py:333
  12.0 0.7 pad_maximum_fusion.5.send_ref
  12.7 11.6 %shard_map.77 = f32[4,24,256]{2,1,0:T(8,128)} custom-call(f32[4,24,256]{2,1,0:T(8,128)} %pad_maximum_fusion.5.send_ref), custom_call_target="tpu_custom_call" | custom-call | tf_op jit(solution)/shard_map/pallas_call | solution.py:312
  24.2 0.7 slice_bitcast_fusion.27
  24.9 0.7 slice_bitcast_fusion.31
  25.6 0.7 slice_bitcast_fusion.39
  26.5 0.7 fusion.115
  27.5 0.7 slice_bitcast_fusion.35
  28.5 2.0 %convolution_bitcast_fusion.7 = f32[4,2,2,8,32,4]{4,5,1,3,2,0:T(4,128)S(1)} fusion(f32[4,2,2,8,256]{4,1,3,2,0:T(2,128)S(1)} %copy.524, f32[4,2,8,4,256]{4,3,2,1,0:T(4,128)S(1)} %pad_maximum_fusion, f32[1,2,8,32,256]{4,3,2,1,0:T(8,128)S(1)} %get-tuple-element.140, f32[1,2,8,32,256]{4,3,2,1,0:T(8,128)S(1)} %get-tuple-element.141, ...), kind=kOutput, calls=%fused_computation.16 | convolution fusion | flops 52035584 | bytes 2555904 | tf_op jit(solution)/shard_map/kcabqs,kabis->kcabiq/dot_general | solution.py:387
  32.2 0.8 neg.91.d_ref.r_ref
  34.6 2.7 %fusion.6 = f32[4,2,2,8,256]{4,1,3,2,0:T(2,128)S(1)} fusion(f32[1,2,2,8,32,4]{4,5,1,3,2,0:T(4,128)S(1)} %get-tuple-element.33, f32[1,2,2,8,32,4]{4,5,1,3,2,0:T(4,128)S(1)} %bitcast.590, f32[1,2,2,8,32,4]{4,5,1,3,2,0:T(4,128)S(1)} %bitcast.574, f32[1,2,2,8,32,4]{4,5,1,3,2,0:T(4,128)S(1)} %bitcast.593, f32[4,2,8,4,256]{4,3,2,1,0:T(4,128)S(1)} %pad_maximum_fusion, ...), kind=kOutput, calls=%fused_computation.11 | convolution fusion | flops 52183040 | bytes 2555904 | tf_op jit(solution)/shard_map/kcabiq,kabis->kcabqs/dot_general | solution.py:333
  38.3 8.5 %shard_map.78 = f32[4,24,256]{2,1,0:T(8,128)} custom-call(f32[4,24,256]{2,1,0:T(8,128)} %pad_maximum_fusion.6.send_ref), custom_call_target="tpu_custom_call" | custom-call | tf_op jit(solution)/shard_map/pallas_call | solution.py:312
  46.7 0.7 slice_bitcast_fusion.25
  47.5 0.7 slice_bitcast_fusion.30
  48.3 0.8 fusion.114
  49.5 0.7 slice_bitcast_fusion.34
  50.3 2.0 %convolution_bitcast_fusion.6 = f32[4,2,2,8,32,4]{4,5,1,3,2,0:T(4,128)S(1)} fusion(f32[4,2,8,4,256]{4,3,2,1,0:T(4,128)S(1)} %pad_maximum_fusion, f32[1,2,8,32,256]{4,3,2,1,0:T(8,128)S(1)} %get-tuple-element.140, f32[1,2,8,32,256]{4,3,2,1,0:T(8,128)S(1)} %copy-done.2, f32[1,2,8,32,256]{4,3,2,1,0:T(8,128)S(1)} %copy-done.4, ...), kind=kOutput, calls=%fused_computation.15 | convolution fusion | flops 52035584 | bytes 2555904 | tf_op jit(solution)/shard_map/kcabqs,kabis->kcabiq/dot_general | solution.py:387
  53.8 0.8 reshape_reshape.15.h_ref
  54.6 22.5 %shard_map.79 = (f32[128,256]{1,0:T(8,128)}, f32[128,256]{1,0:T(8,128)}, f32[128,256]{1,0:T(8,128)}, f32[8,128]{1,0:T(8,128)}) custom-call(f32[128,256]{1,0:T(8,128)} %neg.91.d_ref.r_ref, f32[128,256]{1,0:T(8,128)} %reshape_reshape.15.h_ref, f32[128,256]{1,0:T(8,128)} %neg.91.d_ref.r_ref), custom_call_target="tpu_custom_call" | custom-call | tf_op jit(solution)/shard_map/pallas_call | solution.py:156
  77.1 1.1 reshape_reshape.16
  78.2 0.7 slice.614
  80.3 1.7 %fusion.5 = f32[4,2,2,8,256]{4,1,3,2,0:T(2,128)S(1)} fusion(f32[1,2,2,8,32,4]{4,5,1,3,2,0:T(4,128)S(1)} %bitcast.588, f32[1,2,2,8,32,4]{4,5,1,3,2,0:T(4,128)S(1)} %bitcast.591, f32[1,2,2,8,32,4]{4,5,1,3,2,0:T(4,128)S(1)} %bitcast.575, f32[1,2,2,8,32,4]{4,5,1,3,2,0:T(4,128)S(1)} %bitcast.594, f32[4,2,8,4,256]{4,3,2,1,0:T(4,128)S(1)} %pad_maximum_fusion, ...), kind=kOutput, calls=%fused_computation.10 | convolution fusion | flops 52183040 | bytes 2555904 | tf_op jit(solution)/shard_map/kcabiq,kabis->kcabqs/dot_general | solution.py:333
  83.5 6.4 %shard_map.80 = f32[4,24,256]{2,1,0:T(8,128)} custom-call(f32[4,24,256]{2,1,0:T(8,128)} %pad_maximum_fusion.7.send_ref), custom_call_target="tpu_custom_call" | custom-call | tf_op jit(solution)/shard_map/pallas_call | solution.py:312
  89.9 0.7 slice_bitcast_fusion.23
  90.6 0.7 slice_bitcast_fusion.29
  91.3 0.7 slice_bitcast_fusion.38
  92.1 0.7 fusion.113
  93.0 0.7 slice_bitcast_fusion.33
  94.0 2.0 %convolution_bitcast_fusion.5 = f32[4,2,2,8,32,4]{4,5,1,3,2,0:T(4,128)S(1)} fusion(f32[4,2,2,8,256]{4,1,3,2,0:T(2,128)S(1)} %copy.575, f32[4,2,8,4,256]{4,3,2,1,0:T(4,128)S(1)} %pad_maximum_fusion, f32[1,2,8,32,256]{4,3,2,1,0:T(8,128)S(1)} %get-tuple-element.140, f32[1,2,8,32,256]{4,3,2,1,0:T(8,128)S(1)} %copy-done.2, ...), kind=kOutput, calls=%fused_computation.14 | convolution fusion | flops 52035584 | bytes 2555904 | tf_op jit(solution)/shard_map/kcabqs,kabis->kcabiq/dot_general | solution.py:387
  97.4 0.8 reshape_reshape.17.h_ref
  98.3 19.4 %shard_map.81 = (f32[128,256]{1,0:T(8,128)}, f32[128,256]{1,0:T(8,128)}, f32[128,256]{1,0:T(8,128)}, f32[8,128]{1,0:T(8,128)}) custom-call(f32[128,256]{1,0:T(8,128)} %get-tuple-element.12.d_ref, f32[128,256]{1,0:T(8,128)} %reshape_reshape.17.h_ref, f32[128,256]{1,0:T(8,128)} %get-tuple-element.13.r_ref, f32[128,256]{1,0:T(8,128)} %get-tuple-element.14.refs_0_, ...), custom_call_target="tpu_custom_call" | custom-call | tf_op jit(solution)/shard_map/pallas_call | solution.py:156
  117.7 1.1 reshape_reshape.18
  118.8 0.7 slice.642
  120.9 1.7 %fusion.4 = f32[4,2,2,8,256]{4,1,3,2,0:T(2,128)S(1)} fusion(f32[1,2,2,8,32,4]{4,5,1,3,2,0:T(4,128)S(1)} %bitcast.589, f32[1,2,2,8,32,4]{4,5,1,3,2,0:T(4,128)S(1)} %bitcast.592, f32[1,2,2,8,32,4]{4,5,1,3,2,0:T(4,128)S(1)} %bitcast.576, f32[1,2,2,8,32,4]{4,5,1,3,2,0:T(4,128)S(1)} %bitcast.595, f32[4,2,8,4,256]{4,3,2,1,0:T(4,128)S(1)} %pad_maximum_fusion, ...), kind=kOutput, calls=%fused_computation.9 | convolution fusion | flops 52183040 | bytes 2555904 | tf_op jit(solution)/shard_map/kcabiq,kabis->kcabqs/dot_general | solution.py:333
  124.0 6.4 %shard_map.82 = f32[4,24,256]{2,1,0:T(8,128)} custom-call(f32[4,24,256]{2,1,0:T(8,128)} %pad_maximum_fusion.8.send_ref), custom_call_target="tpu_custom_call" | custom-call | tf_op jit(solution)/shard_map/pallas_call | solution.py:312
  130.4 0.7 slice_bitcast_fusion.21
  131.2 0.7 slice_bitcast_fusion.28
  131.9 0.7 slice_bitcast_fusion.37
  132.7 0.7 fusion.112
  133.6 0.7 slice_bitcast_fusion.32
  134.6 2.0 %convolution_bitcast_fusion.4 = f32[4,2,2,8,32,4]{4,5,1,3,2,0:T(4,128)S(1)} fusion(f32[4,2,2,8,256]{4,1,3,2,0:T(2,128)S(1)} %copy.596, f32[4,2,8,4,256]{4,3,2,1,0:T(4,128)S(1)} %pad_maximum_fusion, f32[1,2,8,32,256]{4,3,2,1,0:T(8,128)S(1)} %get-tuple-element.140, f32[1,2,8,32,256]{4,3,2,1,0:T(8,128)S(1)} %copy-done.2, ...), kind=kOutput, calls=%fused_computation.13 | convolution fusion | flops 52035584 | bytes 2555904 | tf_op jit(solution)/shard_map/kcabqs,kabis->kcabiq/dot_general | solution.py:387
  138.0 0.8 reshape_reshape.19.h_ref
  138.9 20.8 %shard_map.83 = (f32[128,256]{1,0:T(8,128)}, f32[128,256]{1,0:T(8,128)}) custom-call(f32[128,256]{1,0:T(8,128)} %get-tuple-element.16.d_ref, f32[128,256]{1,0:T(8,128)} %reshape_reshape.19.h_ref, f32[128,256]{1,0:T(8,128)} %get-tuple-element.17.r_ref, f32[128,256]{1,0:T(8,128)} %get-tuple-element.18.refs_0_, f32[8,128]{1,0:T(8,128)} %get-tuple-element.19.refs_1_), custom_call_target="tpu_custom_call" | custom-call | tf_op jit(solution)/shard_map/pallas_call | solution.py:156
  159.6 1.6 add.434
  161.2 1.6 copy.842
  (313 shorter events, 22.6 us)
Async XLA Ops:
  2.7 0.8 copy-start.10
  4.6 1.3 copy-start.9
  4.9 1.1 copy-start.11
  6.1 0.8 copy-start.12
  7.4 21.1 %copy-start.1 = (f32[1,2,8,32,256]{4,3,2,1,0:T(8,128)}, f32[1,2,8,32,256]{4,3,2,1,0:T(8,128)S(1)}, u32[]{:S(2)}) copy-start(f32[1,2,8,32,256]{4,3,2,1,0:T(8,128)S(1)} %get-tuple-element.141) | copy-start | bytes 1572868
  7.5 0.9 copy-start.13
  7.5 1.0 copy-start.14
  7.8 20.6 %copy-start.3 = (f32[1,2,8,32,256]{4,3,2,1,0:T(8,128)}, f32[1,2,8,32,256]{4,3,2,1,0:T(8,128)S(1)}, u32[]{:S(2)}) copy-start(f32[1,2,8,32,256]{4,3,2,1,0:T(8,128)S(1)} %get-tuple-element.142) | copy-start | bytes 1572868
  7.8 20.6 %copy-start.5 = (f32[1,2,8,32,256]{4,3,2,1,0:T(8,128)}, f32[1,2,8,32,256]{4,3,2,1,0:T(8,128)S(1)}, u32[]{:S(2)}) copy-start(f32[1,2,8,32,256]{4,3,2,1,0:T(8,128)S(1)} %get-tuple-element.143) | copy-start | bytes 1572868
  10.2 0.7 copy-start.24
  11.0 0.5 copy-start.20
  11.9 25.6 %copy-start.17 = (f32[6]{0:T(128)}, f32[6]{0:T(128)S(1)}, u32[]{:S(2)}) copy-start(f32[6]{0:T(128)S(1)} %pad.234.clone) | copy-start | bytes 76
  33.4 1.0 copy-start.2
  33.4 1.2 copy-start.4
  34.6 2.8 %copy-start.21 = (f32[24]{0:T(128)S(1)}, f32[24]{0:T(128)}, u32[]{:S(2)}) copy-start(f32[24]{0:T(128)} %copy-done.20) | copy-start | bytes 292
  48.2 2.1 %copy-start.6 = (f32[1,2,8,32,256]{4,3,2,1,0:T(8,128)S(1)}, f32[1,2,8,32,256]{4,3,2,1,0:T(8,128)}, u32[]{:S(2)}) copy-start(f32[1,2,8,32,256]{4,3,2,1,0:T(8,128)} %copy-done.5) | copy-start | bytes 1572868
  79.1 1.0 copy-start.7
  79.4 0.9 copy-start.15
  80.3 1.8 %copy-start.22 = (f32[24]{0:T(128)S(1)}, f32[24]{0:T(128)}, u32[]{:S(2)}) copy-start(f32[24]{0:T(128)} %copy-done.20) | copy-start | bytes 292
  82.1 0.7 copy-start.18
  119.7 1.0 copy-start.8
  120.0 0.9 copy-start.16
  120.9 1.8 %copy-start.23 = (f32[24]{0:T(128)S(1)}, f32[24]{0:T(128)}, u32[]{:S(2)}) copy-start(f32[24]{0:T(128)} %copy-done.20) | copy-start | bytes 292
  122.6 0.7 copy-start.19
  138.0 21.6 %copy-start = (f32[2,64,256]{2,1,0:T(8,128)S(1)}, f32[2,64,256]{2,1,0:T(8,128)}, u32[]{:S(2)}) copy-start(f32[2,64,256]{2,1,0:T(8,128)} %param.6) | copy-start | bytes 393220

commit v3 on v2

--- a/solution.py
+++ b/solution.py
@@ -24,7 +24,7 @@
         u_ref, rr_ref = refs[:2]
         refs = refs[2:]
     if last:
-        u_out, r_out, row_buf, col_buf, mine, part, row_send, row_recv, col_send, col_recv = refs
+        image_out, step_out, row_buf, col_buf, mine, part, row_send, row_recv, col_send, col_recv = refs
     else:
         (u_out, r_out, d_out, rr_out, row_buf, col_buf, mine, part, row_send, row_recv, col_send,
          col_recv) = refs
@@ -125,6 +125,10 @@
     curv = pick(0)
     norm_now = pick(len(parts) - 1) if first else rr_ref[0:1, 0:1]
     step_size = norm_now / curv
+    if last:
+        image_out[...] = image
+        step_out[...] = jnp.broadcast_to(step_size, (8, 128))
+        return
     if first:
         u_out[...] = step_size * direction
     else:
@@ -150,9 +154,8 @@
     if not first:
         fields += [update.reshape(flat), norm_tile]
     field_type = jax.ShapeDtypeStruct(flat, jnp.float32)
-    out_shape = [field_type, field_type]
-    if not last:
-        out_shape += [field_type, jax.ShapeDtypeStruct((8, 128), jnp.float32)]
+    tile_type = jax.ShapeDtypeStruct((8, 128), jnp.float32)
+    out_shape = [field_type, tile_type] if last else [field_type, field_type, field_type, tile_type]
     got = pl.pallas_call(
         functools.partial(_cg_kernel, names, first, last),
         out_shape=tuple(out_shape),
@@ -172,10 +175,13 @@
             collective_id=10 + iteration, has_side_effects=True
         ),
     )(*fields)
+    if last:
+        step_size = got[1][0, 0]
+        update = update + step_size * direction
+        residual = residual - step_size * got[0].reshape(shape)
+        return update, residual, None, None
     update = got[0].reshape(shape)
     residual = got[1].reshape(shape)
-    if last:
-        return update, residual, None, None
     return update, residual, got[2].reshape(shape), got[3]
 
 

time: 165 us -> 165 us (level)
    unnamed x99 -> x106, local copies, waits for them, and re-layouts: 11.4 us -> 9.97 us
where the time goes in v3:
time: 165 us; the launch traced here: 164 us
  Pallas kernels  95.3 us (58%)
  local copies, waits for them, and re-layouts  38.2 us (23%)
  matrix products  15.9 us (10%)
  other arithmetic  12 us (7%)
  between operations  2.19 us (1%)
    pallas_call x3, Pallas kernels, cg_step(): pl.pallas_call(functools.partial(_cg_kernel, names, first, last), out_sha...  62.5 us
    pallas_call x4, Pallas kernels, halo_exchange(): pl.pallas_call(functools.partial(_halo_kernel, names), out_shape=jax.Shap...  32.8 us
    unnamed x106, local copies, waits for them, and re-layouts  9.97 us
    dot_general x4, matrix products, seam_term(): jnp.einsum('kcabqs,kabis->kcabiq', weighted, along_table, precision=lax.P...  7.94 us
    dot_general x4, matrix products, seam_term(): jnp.einsum('kcabiq,kabis->kcabqs', bands, along_table, precision=lax.Prec...  7.92 us

profile of v3, /device:TPU:1, one launch (start us, length us, event | category | flops | bytes accessed | tf_op | source)
XLA Modules:
  0.0 163.5 jit_solution(3129507750749175015)
XLA Ops:
  0.6 1.1 reshape.853
  3.6 0.7 slice.538
  5.1 0.7 slice.535
  8.5 1.7 %fusion.7 = f32[4,2,2,8,256]{4,1,3,2,0:T(2,128)S(1)} fusion(f32[1,2,2,8,32,4]{4,5,1,3,2,0:T(4,128)S(1)} %bitcast.586, f32[1,2,2,8,32,4]{4,5,1,3,2,0:T(4,128)S(1)} %bitcast.587, f32[1,2,2,8,32,4]{4,5,1,3,2,0:T(4,128)S(1)} %bitcast.574, f32[1,2,2,8,32,4]{4,5,1,3,2,0:T(4,128)S(1)} %bitcast.588, f32[4,2,8,4,256]{4,3,2,1,0:T(4,128)S(1)} %pad_maximum_fusion, ...), kind=kOutput, calls=%fused_computation.12 | convolution fusion | flops 52183040 | bytes 2555904 | tf_op jit(solution)/shard_map/kcabiq,kabis->kcabqs/dot_general | solution.py:339
  12.7 11.5 %shard_map.77 = f32[4,24,256]{2,1,0:T(8,128)} custom-call(f32[4,24,256]{2,1,0:T(8,128)} %pad_maximum_fusion.5.send_ref), custom_call_target="tpu_custom_call" | custom-call | tf_op jit(solution)/shard_map/pallas_call | solution.py:318
  24.3 0.7 slice_bitcast_fusion.27
  25.0 0.7 slice_bitcast_fusion.31
  25.7 0.7 slice_bitcast_fusion.39
  26.5 0.7 fusion.115
  27.5 0.7 slice_bitcast_fusion.35
  28.5 2.0 %convolution_bitcast_fusion.7 = f32[4,2,2,8,32,4]{4,5,1,3,2,0:T(4,128)S(1)} fusion(f32[4,2,2,8,256]{4,1,3,2,0:T(2,128)S(1)} %copy.524, f32[4,2,8,4,256]{4,3,2,1,0:T(4,128)S(1)} %pad_maximum_fusion, f32[1,2,8,32,256]{4,3,2,1,0:T(8,128)S(1)} %get-tuple-element.140, f32[1,2,8,32,256]{4,3,2,1,0:T(8,128)S(1)} %get-tuple-element.141, ...), kind=kOutput, calls=%fused_computation.16 | convolution fusion | flops 52035584 | bytes 2555904 | tf_op jit(solution)/shard_map/kcabqs,kabis->kcabiq/dot_general | solution.py:393
  32.2 0.8 neg.91.d_ref.r_ref
  34.6 2.7 %fusion.6 = f32[4,2,2,8,256]{4,1,3,2,0:T(2,128)S(1)} fusion(f32[1,2,2,8,32,4]{4,5,1,3,2,0:T(4,128)S(1)} %get-tuple-element.33, f32[1,2,2,8,32,4]{4,5,1,3,2,0:T(4,128)S(1)} %bitcast.591, f32[1,2,2,8,32,4]{4,5,1,3,2,0:T(4,128)S(1)} %bitcast.575, f32[1,2,2,8,32,4]{4,5,1,3,2,0:T(4,128)S(1)} %bitcast.594, f32[4,2,8,4,256]{4,3,2,1,0:T(4,128)S(1)} %pad_maximum_fusion, ...), kind=kOutput, calls=%fused_computation.11 | convolution fusion | flops 52183040 | bytes 2555904 | tf_op jit(solution)/shard_map/kcabiq,kabis->kcabqs/dot_general | solution.py:339
  38.3 8.5 %shard_map.78 = f32[4,24,256]{2,1,0:T(8,128)} custom-call(f32[4,24,256]{2,1,0:T(8,128)} %pad_maximum_fusion.6.send_ref), custom_call_target="tpu_custom_call" | custom-call | tf_op jit(solution)/shard_map/pallas_call | solution.py:318
  46.8 0.7 slice_bitcast_fusion.25
  47.5 0.7 slice_bitcast_fusion.30
  48.4 0.8 fusion.114
  49.6 0.7 slice_bitcast_fusion.34
  50.4 2.0 %convolution_bitcast_fusion.6 = f32[4,2,2,8,32,4]{4,5,1,3,2,0:T(4,128)S(1)} fusion(f32[4,2,8,4,256]{4,3,2,1,0:T(4,128)S(1)} %pad_maximum_fusion, f32[1,2,8,32,256]{4,3,2,1,0:T(8,128)S(1)} %get-tuple-element.140, f32[1,2,8,32,256]{4,3,2,1,0:T(8,128)S(1)} %copy-done.3, f32[1,2,8,32,256]{4,3,2,1,0:T(8,128)S(1)} %copy-done.5, ...), kind=kOutput, calls=%fused_computation.15 | convolution fusion | flops 52035584 | bytes 2555904 | tf_op jit(solution)/shard_map/kcabqs,kabis->kcabiq/dot_general | solution.py:393
  53.8 0.8 reshape_reshape.15.h_ref
  54.7 22.5 %shard_map.79 = (f32[128,256]{1,0:T(8,128)}, f32[128,256]{1,0:T(8,128)}, f32[128,256]{1,0:T(8,128)}, f32[8,128]{1,0:T(8,128)}) custom-call(f32[128,256]{1,0:T(8,128)} %neg.91.d_ref.r_ref, f32[128,256]{1,0:T(8,128)} %reshape_reshape.15.h_ref, f32[128,256]{1,0:T(8,128)} %neg.91.d_ref.r_ref), custom_call_target="tpu_custom_call" | custom-call | tf_op jit(solution)/shard_map/pallas_call | solution.py:159
  77.2 1.1 reshape_reshape.16
  78.3 0.7 slice.617
  80.4 1.7 %fusion.5 = f32[4,2,2,8,256]{4,1,3,2,0:T(2,128)S(1)} fusion(f32[1,2,2,8,32,4]{4,5,1,3,2,0:T(4,128)S(1)} %bitcast.589, f32[1,2,2,8,32,4]{4,5,1,3,2,0:T(4,128)S(1)} %bitcast.592, f32[1,2,2,8,32,4]{4,5,1,3,2,0:T(4,128)S(1)} %bitcast.576, f32[1,2,2,8,32,4]{4,5,1,3,2,0:T(4,128)S(1)} %bitcast.595, f32[4,2,8,4,256]{4,3,2,1,0:T(4,128)S(1)} %pad_maximum_fusion, ...), kind=kOutput, calls=%fused_computation.10 | convolution fusion | flops 52183040 | bytes 2555904 | tf_op jit(solution)/shard_map/kcabiq,kabis->kcabqs/dot_general | solution.py:339
  83.5 6.4 %shard_map.80 = f32[4,24,256]{2,1,0:T(8,128)} custom-call(f32[4,24,256]{2,1,0:T(8,128)} %pad_maximum_fusion.7.send_ref), custom_call_target="tpu_custom_call" | custom-call | tf_op jit(solution)/shard_map/pallas_call | solution.py:318
  89.9 0.7 slice_bitcast_fusion.23
  90.7 0.7 slice_bitcast_fusion.29
  91.4 0.7 slice_bitcast_fusion.38
  92.2 0.7 fusion.113
  93.1 0.7 slice_bitcast_fusion.33
  94.1 2.0 %convolution_bitcast_fusion.5 = f32[4,2,2,8,32,4]{4,5,1,3,2,0:T(4,128)S(1)} fusion(f32[4,2,2,8,256]{4,1,3,2,0:T(2,128)S(1)} %copy.575, f32[4,2,8,4,256]{4,3,2,1,0:T(4,128)S(1)} %pad_maximum_fusion, f32[1,2,8,32,256]{4,3,2,1,0:T(8,128)S(1)} %get-tuple-element.140, f32[1,2,8,32,256]{4,3,2,1,0:T(8,128)S(1)} %copy-done.3, ...), kind=kOutput, calls=%fused_computation.14 | convolution fusion | flops 52035584 | bytes 2555904 | tf_op jit(solution)/shard_map/kcabqs,kabis->kcabiq/dot_general | solution.py:393
  97.5 0.8 reshape_reshape.17.h_ref
  98.4 19.4 %shard_map.81 = (f32[128,256]{1,0:T(8,128)}, f32[128,256]{1,0:T(8,128)}, f32[128,256]{1,0:T(8,128)}, f32[8,128]{1,0:T(8,128)}) custom-call(f32[128,256]{1,0:T(8,128)} %get-tuple-element.12.d_ref, f32[128,256]{1,0:T(8,128)} %reshape_reshape.17.h_ref, f32[128,256]{1,0:T(8,128)} %get-tuple-element.13.r_ref, f32[128,256]{1,0:T(8,128)} %get-tuple-element.14.refs_0_, ...), custom_call_target="tpu_custom_call" | custom-call | tf_op jit(solution)/shard_map/pallas_call | solution.py:159
  117.7 1.1 reshape_reshape.18
  118.9 0.7 slice.645
  121.0 1.7 %fusion.4 = f32[4,2,2,8,256]{4,1,3,2,0:T(2,128)S(1)} fusion(f32[1,2,2,8,32,4]{4,5,1,3,2,0:T(4,128)S(1)} %bitcast.590, f32[1,2,2,8,32,4]{4,5,1,3,2,0:T(4,128)S(1)} %bitcast.593, f32[1,2,2,8,32,4]{4,5,1,3,2,0:T(4,128)S(1)} %bitcast.577, f32[1,2,2,8,32,4]{4,5,1,3,2,0:T(4,128)S(1)} %bitcast.596, f32[4,2,8,4,256]{4,3,2,1,0:T(4,128)S(1)} %pad_maximum_fusion, ...), kind=kOutput, calls=%fused_computation.9 | convolution fusion | flops 52183040 | bytes 2555904 | tf_op jit(solution)/shard_map/kcabiq,kabis->kcabqs/dot_general | solution.py:339
  124.1 6.4 %shard_map.82 = f32[4,24,256]{2,1,0:T(8,128)} custom-call(f32[4,24,256]{2,1,0:T(8,128)} %pad_maximum_fusion.8.send_ref), custom_call_target="tpu_custom_call" | custom-call | tf_op jit(solution)/shard_map/pallas_call | solution.py:318
  130.5 0.7 slice_bitcast_fusion.21
  131.2 0.7 slice_bitcast_fusion.28
  131.9 0.7 slice_bitcast_fusion.37
  132.8 0.7 fusion.112
  133.7 0.7 slice_bitcast_fusion.32
  134.6 2.0 %convolution_bitcast_fusion.4 = f32[4,2,2,8,32,4]{4,5,1,3,2,0:T(4,128)S(1)} fusion(f32[4,2,2,8,256]{4,1,3,2,0:T(2,128)S(1)} %copy.596, f32[4,2,8,4,256]{4,3,2,1,0:T(4,128)S(1)} %pad_maximum_fusion, f32[1,2,8,32,256]{4,3,2,1,0:T(8,128)S(1)} %get-tuple-element.140, f32[1,2,8,32,256]{4,3,2,1,0:T(8,128)S(1)} %copy-done.3, ...), kind=kOutput, calls=%fused_computation.13 | convolution fusion | flops 52035584 | bytes 2555904 | tf_op jit(solution)/shard_map/kcabqs,kabis->kcabiq/dot_general | solution.py:393
  138.1 0.8 reshape_reshape.19.h_ref
  138.9 20.7 %shard_map.83 = (f32[128,256]{1,0:T(8,128)}, f32[8,128]{1,0:T(8,128)}) custom-call(f32[128,256]{1,0:T(8,128)} %get-tuple-element.17.d_ref, f32[128,256]{1,0:T(8,128)} %reshape_reshape.19.h_ref, f32[128,256]{1,0:T(8,128)} %get-tuple-element.18.r_ref, f32[128,256]{1,0:T(8,128)} %get-tuple-element.16.refs_0_, f32[8,128]{1,0:T(8,128)} %get-tuple-element.19.refs_1_), custom_call_target="tpu_custom_call" | custom-call | tf_op jit(solution)/shard_map/pallas_call | solution.py:159
  159.6 1.2 slice.669
  161.6 0.7 add.442
  162.2 1.3 multiply_subtract_fusion
  (323 shorter events, 24.0 us)
Async XLA Ops:
  2.7 0.8 copy-start.14
  4.6 1.3 copy-start.12
  4.9 1.1 copy-start.15
  6.1 0.8 copy-start.16
  7.4 21.1 %copy-start.2 = (f32[1,2,8,32,256]{4,3,2,1,0:T(8,128)}, f32[1,2,8,32,256]{4,3,2,1,0:T(8,128)S(1)}, u32[]{:S(2)}) copy-start(f32[1,2,8,32,256]{4,3,2,1,0:T(8,128)S(1)} %get-tuple-element.141) | copy-start | bytes 1572868
  7.5 0.9 copy-start.17
  7.5 1.0 copy-start.18
  7.8 20.7 %copy-start.4 = (f32[1,2,8,32,256]{4,3,2,1,0:T(8,128)}, f32[1,2,8,32,256]{4,3,2,1,0:T(8,128)S(1)}, u32[]{:S(2)}) copy-start(f32[1,2,8,32,256]{4,3,2,1,0:T(8,128)S(1)} %get-tuple-element.142) | copy-start | bytes 1572868
  7.8 20.7 %copy-start.6 = (f32[1,2,8,32,256]{4,3,2,1,0:T(8,128)}, f32[1,2,8,32,256]{4,3,2,1,0:T(8,128)S(1)}, u32[]{:S(2)}) copy-start(f32[1,2,8,32,256]{4,3,2,1,0:T(8,128)S(1)} %get-tuple-element.143) | copy-start | bytes 1572868
  10.2 0.7 copy-start.28
  11.0 0.6 copy-start.24
  12.0 25.6 %copy-start.21 = (f32[6]{0:T(128)}, f32[6]{0:T(128)S(1)}, u32[]{:S(2)}) copy-start(f32[6]{0:T(128)S(1)} %pad.234.clone) | copy-start | bytes 76
  33.4 1.0 copy-start.3
  33.4 1.2 copy-start.5
  34.6 2.8 %copy-start.25 = (f32[24]{0:T(128)S(1)}, f32[24]{0:T(128)}, u32[]{:S(2)}) copy-start(f32[24]{0:T(128)} %copy-done.24) | copy-start | bytes 292
  48.2 2.1 %copy-start.7 = (f32[1,2,8,32,256]{4,3,2,1,0:T(8,128)S(1)}, f32[1,2,8,32,256]{4,3,2,1,0:T(8,128)}, u32[]{:S(2)}) copy-start(f32[1,2,8,32,256]{4,3,2,1,0:T(8,128)} %copy-done.6) | copy-start | bytes 1572868
  79.2 1.0 copy-start.8
  79.5 0.9 copy-start.19
  80.4 1.8 %copy-start.26 = (f32[24]{0:T(128)S(1)}, f32[24]{0:T(128)}, u32[]{:S(2)}) copy-start(f32[24]{0:T(128)} %copy-done.24) | copy-start | bytes 292
  82.1 0.7 copy-start.22
  119.8 1.0 copy-start.9
  120.1 0.9 copy-start.20
  121.0 1.8 %copy-start.27 = (f32[24]{0:T(128)S(1)}, f32[24]{0:T(128)}, u32[]{:S(2)}) copy-start(f32[24]{0:T(128)} %copy-done.24) | copy-start | bytes 292
  122.7 0.7 copy-start.23
  138.1 22.8 %copy-start = (f32[128,256]{1,0:T(8,128)S(1)}, f32[128,256]{1,0:T(8,128)}, u32[]{:S(2)}) copy-start(f32[128,256]{1,0:T(8,128)} %get-tuple-element.17.d_ref) | copy-start | bytes 393220
  138.1 22.8 %copy-start.11 = (f32[128,256]{1,0:T(8,128)S(1)}, f32[128,256]{1,0:T(8,128)}, u32[]{:S(2)}) copy-start(f32[128,256]{1,0:T(8,128)} %get-tuple-element.16.refs_0_) | copy-start | bytes 393220
  138.9 22.6 %copy-start.1 = (f32[2,64,256]{2,1,0:T(8,128)S(1)}, f32[2,64,256]{2,1,0:T(8,128)}, u32[]{:S(2)}) copy-start(f32[2,64,256]{2,1,0:T(8,128)} %param.6) | copy-start | bytes 393220
  159.6 2.6 %copy-start.10 = (f32[128,256]{1,0:T(8,128)S(1)}, f32[128,256]{1,0:T(8,128)}, u32[]{:S(2)}) copy-start(f32[128,256]{1,0:T(8,128)} %get-tuple-element.18.r_ref) | copy-start | bytes 393220
  159.6 2.6 %copy-start.13 = (f32[128,256]{1,0:T(8,128)S(1)}, f32[128,256]{1,0:T(8,128)}, u32[]{:S(2)}) copy-start(f32[128,256]{1,0:T(8,128)} %get-tuple-element.21) | copy-start | bytes 393220

commit v4 on v2

--- a/solution.py
+++ b/solution.py
@@ -271,7 +271,8 @@
     return result.reshape(control.shape)
 
 
-def _halo_kernel(names, send_ref, recv_ref, send_sems, recv_sems):
+def _halo_kernel(names, *refs):
+    send_refs, recv_refs, (send_sems, recv_sems) = refs[:4], refs[4:8], refs[8:]
     ncol = lax.axis_size("col")
     nrow = lax.axis_size("row")
     ci = lax.axis_index("col")
@@ -293,7 +294,7 @@
     pl.semaphore_wait(barrier, len(peers))
     copies = [
         pltpu.make_async_remote_copy(
-            src_ref=send_ref.at[k], dst_ref=recv_ref.at[k], send_sem=send_sems.at[k],
+            src_ref=send_refs[k], dst_ref=recv_refs[k], send_sem=send_sems.at[k],
             recv_sem=recv_sems.at[k], device_id=peers[k], device_id_type=MESH_ID)
         for k in range(4)
     ]
@@ -306,18 +307,15 @@
 
 def halo_exchange(names, to_east, to_west, to_south, to_north):
     slabs = [to_east, to_west, to_south, to_north]
-    rows = max(slab.shape[0] for slab in slabs)
-    lanes = slabs[0].shape[1]
-    stacked = jnp.stack([jnp.pad(slab, ((0, rows - slab.shape[0]), (0, 0))) for slab in slabs])
     got = pl.pallas_call(
         functools.partial(_halo_kernel, names),
-        out_shape=jax.ShapeDtypeStruct(stacked.shape, jnp.float32),
-        in_specs=[pl.BlockSpec(memory_space=pltpu.VMEM)],
-        out_specs=pl.BlockSpec(memory_space=pltpu.VMEM),
+        out_shape=tuple(jax.ShapeDtypeStruct(slab.shape, jnp.float32) for slab in slabs),
+        in_specs=[pl.BlockSpec(memory_space=pltpu.VMEM)] * 4,
+        out_specs=tuple(pl.BlockSpec(memory_space=pltpu.VMEM) for _ in slabs),
         scratch_shapes=[pltpu.SemaphoreType.DMA((4,)), pltpu.SemaphoreType.DMA((4,))],
         compiler_params=pltpu.CompilerParams(collective_id=1, has_side_effects=True),
-    )(stacked)
-    return [got[k, : slabs[k].shape[0]] for k in range(4)]
+    )(*slabs)
+    return list(got)
 
 
 def all_weight_tables(tables):

time: 165 us -> 167 us (1.012)
  other arithmetic: 10.9 us -> 14.6 us
    mul x8 -> x0, local copies, waits for them, and re-layouts: 5.59 us -> none  [the longest x4 2.8 us: seam_term(): from_west = (west_east - seam_values[1][:, :, :1]) * west_mask]
    another operation x8 -> x0, other arithmetic: 2.9 us -> none  [halo_exchange(): jnp.stack([jnp.pad(slab, ((0, rows - slab.shape[0]), (0, 0))) for slab in...]
    slice x4, local copies, waits for them, and re-layouts: 2.9 us -> 0.01 us  [seam_term(): west_east = got_west[:2 * tile_rows].reshape(2, tile_rows, 1, samples)]
    reshape x0 -> x10, local copies, waits for them, and re-layouts: none -> 2.88 us  [the longest x8 1.43 us: seam_term(): east_next = got_east.reshape(2, tile_rows, 1, samples)]
    slice x0 -> x8, local copies, waits for them, and re-layouts: none -> 2.82 us  [the longest x4 2.81 us: seam_term(): north_mask = got_north[2 * tile_cols:].reshape(1, 1, tile_cols, samples)]
    concatenate x0 -> x4, other arithmetic: none -> 2.72 us  [seam_term(): jnp.concatenate([own_south[:, -1].reshape(2 * tile_cols, samples), jnp.br...]
    concatenate x4, other arithmetic: 0.28 us -> 2.66 us  [seam_term(): jnp.concatenate([own_east[:, :, -1].reshape(2 * tile_rows, samples), jnp....]
    another operation x4, local copies, waits for them, and re-layouts: 0.06 us -> 2.42 us  [seam_term(): to_west = seam_values[1][:, :, 0].reshape(2 * tile_rows, samples)]
where the time goes in v4:
time: 167 us; the launch traced here: 165 us
  Pallas kernels  94.2 us (56%)
  local copies, waits for them, and re-layouts  38.3 us (23%)
  matrix products  15.9 us (10%)
  other arithmetic  14.6 us (9%)
  between operations  2.15 us (1%)
    pallas_call x3, Pallas kernels, cg_step(): pl.pallas_call(functools.partial(_cg_kernel, names, first, last), out_sha...  62.2 us
    pallas_call x4, Pallas kernels, halo_exchange(): pl.pallas_call(functools.partial(_halo_kernel, names), out_shape=tuple((j...  32 us
    unnamed x117, local copies, waits for them, and re-layouts  10.2 us
    dot_general x4, matrix products, seam_term(): jnp.einsum('kcabqs,kabis->kcabiq', weighted, along_table, precision=lax.P...  7.94 us
    dot_general x4, matrix products, seam_term(): jnp.einsum('kcabiq,kabis->kcabqs', bands, along_table, precision=lax.Prec...  7.92 us

profile of v4, /device:TPU:1, one launch (start us, length us, event | category | flops | bytes accessed | tf_op | source)
XLA Modules:
  0.0 165.1 jit_solution(13487484857743660899)
XLA Ops:
  0.6 1.1 reshape.841
  3.6 0.7 slice.471
  5.1 0.7 slice.468
  8.5 1.7 %fusion.7 = f32[4,2,2,8,256]{4,1,3,2,0:T(2,128)S(1)} fusion(f32[1,2,2,8,32,4]{4,5,1,3,2,0:T(4,128)S(1)} %bitcast.529, f32[1,2,2,8,32,4]{4,5,1,3,2,0:T(4,128)S(1)} %bitcast.530, f32[1,2,2,8,32,4]{4,5,1,3,2,0:T(4,128)S(1)} %bitcast.517, f32[1,2,2,8,32,4]{4,5,1,3,2,0:T(4,128)S(1)} %bitcast.531, f32[4,2,8,4,256]{4,3,2,1,0:T(4,128)S(1)} %pad_maximum_fusion, ...), kind=kOutput, calls=%fused_computation.12 | convolution fusion | flops 52183040 | bytes 2555904 | tf_op jit(solution)/shard_map/kcabiq,kabis->kcabqs/dot_general | solution.py:331
  12.6 0.7 pad_maximum_fusion.7.refs_2_
  13.9 11.4 %shard_map.77 = (f32[6,256]{1,0:T(8,128)}, f32[4,256]{1,0:T(4,128)}, f32[24,256]{1,0:T(8,128)}, f32[16,256]{1,0:T(8,128)}) custom-call(f32[6,256]{1,0:T(8,128)} %pad_maximum_fusion.15.refs_0_, f32[4,256]{1,0:T(4,128)} %reshape_squeeze.49.refs_1_, f32[24,256]{1,0:T(8,128)} %pad_maximum_fusion.7.refs_2_, f32[16,256]{1,0:T(8,128)} %slice_bitcast_fusion.19.refs_3_), custom_call_target="tpu_custom_call" | custom-call | tf_op jit(solution)/shard_map/pallas_call | solution.py:310
  25.3 0.7 slice.501
  26.0 0.7 slice_bitcast_fusion.23
  26.9 0.7 concatenate.219
  28.2 2.0 %convolution_bitcast_fusion.7 = f32[4,2,2,8,32,4]{4,5,1,3,2,0:T(4,128)S(1)} fusion(f32[4,2,2,8,256]{4,1,3,2,0:T(2,128)S(1)} %copy.524, f32[4,2,8,4,256]{4,3,2,1,0:T(4,128)S(1)} %pad_maximum_fusion, f32[1,2,8,32,256]{4,3,2,1,0:T(8,128)S(1)} %get-tuple-element.155, f32[1,2,8,32,256]{4,3,2,1,0:T(8,128)S(1)} %get-tuple-element.156, ...), kind=kOutput, calls=%fused_computation.16 | convolution fusion | flops 52035584 | bytes 2555904 | tf_op jit(solution)/shard_map/kcabqs,kabis->kcabiq/dot_general | solution.py:385
  31.9 0.8 neg.91.d_ref.r_ref
  34.2 2.7 %fusion.6 = f32[4,2,2,8,256]{4,1,3,2,0:T(2,128)S(1)} fusion(f32[1,2,2,8,32,4]{4,5,1,3,2,0:T(4,128)S(1)} %get-tuple-element.65, f32[1,2,2,8,32,4]{4,5,1,3,2,0:T(4,128)S(1)} %bitcast.534, f32[1,2,2,8,32,4]{4,5,1,3,2,0:T(4,128)S(1)} %bitcast.518, f32[1,2,2,8,32,4]{4,5,1,3,2,0:T(4,128)S(1)} %bitcast.537, f32[4,2,8,4,256]{4,3,2,1,0:T(4,128)S(1)} %pad_maximum_fusion, ...), kind=kOutput, calls=%fused_computation.11 | convolution fusion | flops 52183040 | bytes 2555904 | tf_op jit(solution)/shard_map/kcabiq,kabis->kcabqs/dot_general | solution.py:331
  38.3 0.7 pad_maximum_fusion.8.refs_2_
  39.6 8.1 %shard_map.78 = (f32[6,256]{1,0:T(8,128)}, f32[4,256]{1,0:T(4,128)}, f32[24,256]{1,0:T(8,128)}, f32[16,256]{1,0:T(8,128)}) custom-call(f32[6,256]{1,0:T(8,128)} %pad_maximum_fusion.16.refs_0_, f32[4,256]{1,0:T(4,128)} %reshape_squeeze.53.refs_1_, f32[24,256]{1,0:T(8,128)} %pad_maximum_fusion.8.refs_2_, f32[16,256]{1,0:T(8,128)} %bitcast.546), custom_call_target="tpu_custom_call" | custom-call | tf_op jit(solution)/shard_map/pallas_call | solution.py:310
  47.7 0.7 copy.548
  48.5 0.7 slice.536
  49.2 0.7 slice_bitcast_fusion.16
  50.0 0.7 concatenate.235
  50.8 0.7 copy.545
  52.0 2.0 %convolution_bitcast_fusion.6 = f32[4,2,2,8,32,4]{4,5,1,3,2,0:T(4,128)S(1)} fusion(f32[4,2,8,4,256]{4,3,2,1,0:T(4,128)S(1)} %pad_maximum_fusion, f32[1,2,8,32,256]{4,3,2,1,0:T(8,128)S(1)} %get-tuple-element.155, f32[1,2,8,32,256]{4,3,2,1,0:T(8,128)S(1)} %copy-done.2, f32[1,2,8,32,256]{4,3,2,1,0:T(8,128)S(1)} %copy-done.4, ...), kind=kOutput, calls=%fused_computation.15 | convolution fusion | flops 52035584 | bytes 2555904 | tf_op jit(solution)/shard_map/kcabqs,kabis->kcabiq/dot_general | solution.py:385
  55.5 0.8 reshape_reshape.15.h_ref
  56.3 22.3 %shard_map.79 = (f32[128,256]{1,0:T(8,128)}, f32[128,256]{1,0:T(8,128)}, f32[128,256]{1,0:T(8,128)}, f32[8,128]{1,0:T(8,128)}) custom-call(f32[128,256]{1,0:T(8,128)} %neg.91.d_ref.r_ref, f32[128,256]{1,0:T(8,128)} %reshape_reshape.15.h_ref, f32[128,256]{1,0:T(8,128)} %neg.91.d_ref.r_ref), custom_call_target="tpu_custom_call" | custom-call | tf_op jit(solution)/shard_map/pallas_call | solution.py:156
  78.6 1.1 reshape_reshape.16
  79.8 0.7 slice.546
  81.9 1.7 %fusion.5 = f32[4,2,2,8,256]{4,1,3,2,0:T(2,128)S(1)} fusion(f32[1,2,2,8,32,4]{4,5,1,3,2,0:T(4,128)S(1)} %bitcast.532, f32[1,2,2,8,32,4]{4,5,1,3,2,0:T(4,128)S(1)} %bitcast.535, f32[1,2,2,8,32,4]{4,5,1,3,2,0:T(4,128)S(1)} %bitcast.519, f32[1,2,2,8,32,4]{4,5,1,3,2,0:T(4,128)S(1)} %bitcast.538, f32[4,2,8,4,256]{4,3,2,1,0:T(4,128)S(1)} %pad_maximum_fusion, ...), kind=kOutput, calls=%fused_computation.10 | convolution fusion | flops 52183040 | bytes 2555904 | tf_op jit(solution)/shard_map/kcabiq,kabis->kcabqs/dot_general | solution.py:331
  85.0 0.7 pad_maximum_fusion.9.refs_2_
  86.3 6.2 %shard_map.80 = (f32[6,256]{1,0:T(8,128)}, f32[4,256]{1,0:T(4,128)}, f32[24,256]{1,0:T(8,128)}, f32[16,256]{1,0:T(8,128)}) custom-call(f32[6,256]{1,0:T(8,128)} %pad_maximum_fusion.17.refs_0_, f32[4,256]{1,0:T(4,128)} %reshape_squeeze.57.refs_1_, f32[24,256]{1,0:T(8,128)} %pad_maximum_fusion.9.refs_2_, f32[16,256]{1,0:T(8,128)} %slice_bitcast_fusion.18.refs_3_), custom_call_target="tpu_custom_call" | custom-call | tf_op jit(solution)/shard_map/pallas_call | solution.py:310
  92.6 0.7 slice.562
  93.3 0.7 slice_bitcast_fusion.22
  94.1 0.8 fusion.62
  94.8 0.7 reshape.851
  96.0 2.0 %convolution_bitcast_fusion.5 = f32[4,2,2,8,32,4]{4,5,1,3,2,0:T(4,128)S(1)} fusion(f32[4,2,2,8,256]{4,1,3,2,0:T(2,128)S(1)} %copy.575, f32[4,2,8,4,256]{4,3,2,1,0:T(4,128)S(1)} %pad_maximum_fusion, f32[1,2,8,32,256]{4,3,2,1,0:T(8,128)S(1)} %get-tuple-element.155, f32[1,2,8,32,256]{4,3,2,1,0:T(8,128)S(1)} %copy-done.2, ...), kind=kOutput, calls=%fused_computation.14 | convolution fusion | flops 52035584 | bytes 2555904 | tf_op jit(solution)/shard_map/kcabqs,kabis->kcabiq/dot_general | solution.py:385
  99.4 0.8 reshape_reshape.17.h_ref
  100.3 19.7 %shard_map.81 = (f32[128,256]{1,0:T(8,128)}, f32[128,256]{1,0:T(8,128)}, f32[128,256]{1,0:T(8,128)}, f32[8,128]{1,0:T(8,128)}) custom-call(f32[128,256]{1,0:T(8,128)} %get-tuple-element.36.d_ref, f32[128,256]{1,0:T(8,128)} %reshape_reshape.17.h_ref, f32[128,256]{1,0:T(8,128)} %get-tuple-element.41.r_ref, f32[128,256]{1,0:T(8,128)} %get-tuple-element.42.refs_0_, ...), custom_call_target="tpu_custom_call" | custom-call | tf_op jit(solution)/shard_map/pallas_call | solution.py:156
  120.0 1.1 reshape_reshape.18
  121.1 0.7 slice.572
  123.2 1.7 %fusion.4 = f32[4,2,2,8,256]{4,1,3,2,0:T(2,128)S(1)} fusion(f32[1,2,2,8,32,4]{4,5,1,3,2,0:T(4,128)S(1)} %bitcast.533, f32[1,2,2,8,32,4]{4,5,1,3,2,0:T(4,128)S(1)} %bitcast.536, f32[1,2,2,8,32,4]{4,5,1,3,2,0:T(4,128)S(1)} %bitcast.520, f32[1,2,2,8,32,4]{4,5,1,3,2,0:T(4,128)S(1)} %bitcast.539, f32[4,2,8,4,256]{4,3,2,1,0:T(4,128)S(1)} %pad_maximum_fusion, ...), kind=kOutput, calls=%fused_computation.9 | convolution fusion | flops 52183040 | bytes 2555904 | tf_op jit(solution)/shard_map/kcabiq,kabis->kcabqs/dot_general | solution.py:331
  126.3 0.7 pad_maximum_fusion.10.refs_2_
  127.6 6.3 %shard_map.82 = (f32[6,256]{1,0:T(8,128)}, f32[4,256]{1,0:T(4,128)}, f32[24,256]{1,0:T(8,128)}, f32[16,256]{1,0:T(8,128)}) custom-call(f32[6,256]{1,0:T(8,128)} %pad_maximum_fusion.18.refs_0_, f32[4,256]{1,0:T(4,128)} %reshape_squeeze.61.refs_1_, f32[24,256]{1,0:T(8,128)} %pad_maximum_fusion.10.refs_2_, f32[16,256]{1,0:T(8,128)} %slice_bitcast_fusion.17.refs_3_), custom_call_target="tpu_custom_call" | custom-call | tf_op jit(solution)/shard_map/pallas_call | solution.py:310
  133.9 0.7 slice.588
  134.6 0.7 slice_bitcast_fusion.21
  135.4 0.8 fusion.64
  136.2 0.7 reshape.855
  137.3 2.0 %convolution_bitcast_fusion.4 = f32[4,2,2,8,32,4]{4,5,1,3,2,0:T(4,128)S(1)} fusion(f32[4,2,2,8,256]{4,1,3,2,0:T(2,128)S(1)} %copy.596, f32[4,2,8,4,256]{4,3,2,1,0:T(4,128)S(1)} %pad_maximum_fusion, f32[1,2,8,32,256]{4,3,2,1,0:T(8,128)S(1)} %get-tuple-element.155, f32[1,2,8,32,256]{4,3,2,1,0:T(8,128)S(1)} %copy-done.2, ...), kind=kOutput, calls=%fused_computation.13 | convolution fusion | flops 52035584 | bytes 2555904 | tf_op jit(solution)/shard_map/kcabqs,kabis->kcabiq/dot_general | solution.py:385
  140.8 0.8 reshape_reshape.19.h_ref
  141.6 20.3 %shard_map.83 = (f32[128,256]{1,0:T(8,128)}, f32[128,256]{1,0:T(8,128)}) custom-call(f32[128,256]{1,0:T(8,128)} %get-tuple-element.44.d_ref, f32[128,256]{1,0:T(8,128)} %reshape_reshape.19.h_ref, f32[128,256]{1,0:T(8,128)} %get-tuple-element.49.r_ref, f32[128,256]{1,0:T(8,128)} %get-tuple-element.50.refs_0_, f32[8,128]{1,0:T(8,128)} %get-tuple-element.51.refs_1_), custom_call_target="tpu_custom_call" | custom-call | tf_op jit(solution)/shard_map/pallas_call | solution.py:156
  161.9 1.6 add.410
  163.5 1.6 copy.842
  (312 shorter events, 26.1 us)
Async XLA Ops:
  2.7 0.8 copy-start.10
  4.6 1.3 copy-start.9
  4.9 1.1 copy-start.11
  6.1 0.8 copy-start.12
  7.4 20.8 %copy-start.1 = (f32[1,2,8,32,256]{4,3,2,1,0:T(8,128)}, f32[1,2,8,32,256]{4,3,2,1,0:T(8,128)S(1)}, u32[]{:S(2)}) copy-start(f32[1,2,8,32,256]{4,3,2,1,0:T(8,128)S(1)} %get-tuple-element.156) | copy-start | bytes 1572868
  7.5 0.9 copy-start.13
  7.5 1.0 copy-start.14
  7.8 20.3 %copy-start.3 = (f32[1,2,8,32,256]{4,3,2,1,0:T(8,128)}, f32[1,2,8,32,256]{4,3,2,1,0:T(8,128)S(1)}, u32[]{:S(2)}) copy-start(f32[1,2,8,32,256]{4,3,2,1,0:T(8,128)S(1)} %get-tuple-element.157) | copy-start | bytes 1572868
  7.8 20.3 %copy-start.5 = (f32[1,2,8,32,256]{4,3,2,1,0:T(8,128)}, f32[1,2,8,32,256]{4,3,2,1,0:T(8,128)S(1)}, u32[]{:S(2)}) copy-start(f32[1,2,8,32,256]{4,3,2,1,0:T(8,128)S(1)} %get-tuple-element.158) | copy-start | bytes 1572868
  10.2 0.7 copy-start.33
  11.2 25.8 %copy-start.22 = (f32[6]{0:T(128)}, f32[6]{0:T(128)S(1)}, u32[]{:S(2)}) copy-start(f32[6]{0:T(128)S(1)} %pad.167.clone) | copy-start | bytes 76
  12.6 0.7 copy-start.25
  25.3 2.4 %copy-start.21 = (f32[4,256]{1,0:T(4,128)S(1)}, f32[4,256]{1,0:T(4,128)}, u32[]{:S(2)}) copy-start(f32[4,256]{1,0:T(4,128)} %get-tuple-element.28) | copy-start | bytes 12292
  25.3 2.5 %copy-start.30 = (f32[6,256]{1,0:T(8,128)S(1)}, f32[6,256]{1,0:T(8,128)}, u32[]{:S(2)}) copy-start(f32[6,256]{1,0:T(8,128)} %get-tuple-element.29) | copy-start | bytes 18436
  25.3 2.6 %copy-start.17 = (f32[16,256]{1,0:T(8,128)S(1)}, f32[16,256]{1,0:T(8,128)}, u32[]{:S(2)}) copy-start(f32[16,256]{1,0:T(8,128)} %get-tuple-element.30) | copy-start | bytes 49156
  33.0 1.0 copy-start.2
  33.0 1.2 copy-start.4
  34.2 4.1 %copy-start.26 = (f32[24]{0:T(128)S(1)}, f32[24]{0:T(128)}, u32[]{:S(2)}) copy-start(f32[24]{0:T(128)} %copy-done.25) | copy-start | bytes 292
  47.7 4.1 %copy-start.20 = (f32[4,256]{1,0:T(4,128)S(1)}, f32[4,256]{1,0:T(4,128)}, u32[]{:S(2)}) copy-start(f32[4,256]{1,0:T(4,128)} %get-tuple-element.32) | copy-start | bytes 12292
  47.7 4.2 %copy-start.29 = (f32[6,256]{1,0:T(8,128)S(1)}, f32[6,256]{1,0:T(8,128)}, u32[]{:S(2)}) copy-start(f32[6,256]{1,0:T(8,128)} %get-tuple-element.33) | copy-start | bytes 18436
  49.9 2.1 %copy-start.6 = (f32[1,2,8,32,256]{4,3,2,1,0:T(8,128)S(1)}, f32[1,2,8,32,256]{4,3,2,1,0:T(8,128)}, u32[]{:S(2)}) copy-start(f32[1,2,8,32,256]{4,3,2,1,0:T(8,128)} %copy-done.5) | copy-start | bytes 1572868
  80.7 1.0 copy-start.7
  81.0 0.9 copy-start.15
  81.9 1.8 %copy-start.23 = (f32[6]{0:T(128)S(1)}, f32[6]{0:T(128)}, u32[]{:S(2)}) copy-start(f32[6]{0:T(128)} %copy-done.22) | copy-start | bytes 76
  83.6 1.4 copy-start.27
  92.5 3.1 %copy-start.32 = (f32[6,256]{1,0:T(8,128)S(1)}, f32[6,256]{1,0:T(8,128)}, u32[]{:S(2)}) copy-start(f32[6,256]{1,0:T(8,128)} %get-tuple-element.38) | copy-start | bytes 18436
  92.5 3.2 %copy-start.19 = (f32[4,256]{1,0:T(4,128)S(1)}, f32[4,256]{1,0:T(4,128)}, u32[]{:S(2)}) copy-start(f32[4,256]{1,0:T(4,128)} %get-tuple-element.37) | copy-start | bytes 12292
  122.0 1.0 copy-start.8
  122.3 0.9 copy-start.16
  123.2 1.8 %copy-start.24 = (f32[6]{0:T(128)S(1)}, f32[6]{0:T(128)}, u32[]{:S(2)}) copy-start(f32[6]{0:T(128)} %copy-done.22) | copy-start | bytes 76
  124.9 1.4 copy-start.28
  133.9 3.2 %copy-start.31 = (f32[6,256]{1,0:T(8,128)S(1)}, f32[6,256]{1,0:T(8,128)}, u32[]{:S(2)}) copy-start(f32[6,256]{1,0:T(8,128)} %get-tuple-element.46) | copy-start | bytes 18436
  133.9 3.2 %copy-start.18 = (f32[4,256]{1,0:T(4,128)S(1)}, f32[4,256]{1,0:T(4,128)}, u32[]{:S(2)}) copy-start(f32[4,256]{1,0:T(4,128)} %get-tuple-element.45) | copy-start | bytes 12292
  140.8 21.1 %copy-start = (f32[2,64,256]{2,1,0:T(8,128)S(1)}, f32[2,64,256]{2,1,0:T(8,128)}, u32[]{:S(2)}) copy-start(f32[2,64,256]{2,1,0:T(8,128)} %param.6) | copy-start | bytes 393220

commit v5 on v2

--- a/solution.py
+++ b/solution.py
@@ -331,7 +331,7 @@
     grid_view = tile_view(control, tile_rows, tile_cols, GRID)
     bands = jnp.stack([edge_band(grid_view, facing, BAND) for facing in range(4)])
     partial_sum = jnp.einsum(
-        "kcabiq,kabis->kcabqs", bands, along_table, precision=lax.Precision.HIGHEST
+        "kcabiq,kabis->kcabqs", bands, along_table, precision=lax.Precision.HIGH
     )
     stacked_values = jnp.sum(partial_sum * across_table[:, None], axis=4)
     seam_values = [stacked_values[facing] for facing in range(4)]
@@ -385,7 +385,7 @@
     residuals = jnp.stack([resid_east, resid_west, resid_south, resid_north])
     weighted = residuals[:, :, :, :, None, :] * across_table[:, None]
     spread_parts = jnp.einsum(
-        "kcabqs,kabis->kcabiq", weighted, along_table, precision=lax.Precision.HIGHEST
+        "kcabqs,kabis->kcabiq", weighted, along_table, precision=lax.Precision.HIGH
     )
     summed = (
         place_edge(spread_parts[0], 0, GRID)

time: 165 us -> 158 us (0.958)
  matrix products: 15.9 us -> 9.21 us
    dot_general x4, matrix products: 7.94 us -> 3.83 us  [seam_term(): jnp.einsum('kcabqs,kabis->kcabiq', weighted, along_table, precision=lax.P...]
    dot_general x4, matrix products: 7.92 us -> 5.38 us  [seam_term(): jnp.einsum('kcabiq,kabis->kcabqs', bands, along_table, precision=lax.Prec...]
where the time goes in v5:
time: 158 us; the launch traced here: 156 us
  Pallas kernels  95.2 us (60%)
  local copies, waits for them, and re-layouts  38.6 us (24%)
  other arithmetic  10.9 us (7%)
  matrix products  9.21 us (6%)
  between operations  2.15 us (1%)
    pallas_call x3, Pallas kernels, cg_step(): pl.pallas_call(functools.partial(_cg_kernel, names, first, last), out_sha...  62.4 us
    pallas_call x4, Pallas kernels, halo_exchange(): pl.pallas_call(functools.partial(_halo_kernel, names), out_shape=jax.Shap...  32.8 us
    unnamed x99, local copies, waits for them, and re-layouts  11.4 us
    dot_general x4, matrix products, seam_term(): jnp.einsum('kcabiq,kabis->kcabqs', bands, along_table, precision=lax.Prec...  5.38 us
    dot_general x4, matrix products, seam_term(): jnp.einsum('kcabqs,kabis->kcabiq', weighted, along_table, precision=lax.P...  3.83 us

profile of v5, /device:TPU:1, one launch (start us, length us, event | category | flops | bytes accessed | tf_op | source)
XLA Modules:
  0.0 156.1 jit_solution(4629518139121724088)
XLA Ops:
  0.6 1.1 reshape.849
  3.6 0.7 slice.535
  5.1 0.7 slice.532
  8.5 1.1 fusion.7
  11.4 0.7 pad_maximum_fusion.5.send_ref
  12.0 11.6 %shard_map.77 = f32[4,24,256]{2,1,0:T(8,128)} custom-call(f32[4,24,256]{2,1,0:T(8,128)} %pad_maximum_fusion.5.send_ref), custom_call_target="tpu_custom_call" | custom-call | tf_op jit(solution)/shard_map/pallas_call | solution.py:312
  23.6 0.7 slice_bitcast_fusion.27
  24.3 0.7 slice_bitcast_fusion.31
  25.0 0.7 slice_bitcast_fusion.39
  25.8 0.7 fusion.115
  26.8 0.7 slice_bitcast_fusion.35
  27.8 1.0 convolution_bitcast_fusion.7
  30.5 0.8 neg.91.d_ref.r_ref
  32.9 2.1 %fusion.6 = f32[4,2,2,8,256]{4,1,3,2,0:T(2,128)S(1)} fusion(f32[1,2,2,8,32,4]{4,5,1,3,2,0:T(4,128)S(1)} %get-tuple-element.33, f32[1,2,2,8,32,4]{4,5,1,3,2,0:T(4,128)S(1)} %bitcast.590, f32[1,2,2,8,32,4]{4,5,1,3,2,0:T(4,128)S(1)} %bitcast.574, f32[1,2,2,8,32,4]{4,5,1,3,2,0:T(4,128)S(1)} %bitcast.593, f32[4,2,8,4,256]{4,3,2,1,0:T(4,128)S(1)} %pad_maximum_fusion, ...), kind=kOutput, calls=%fused_computation.11 | convolution fusion | flops 27017216 | bytes 2555904 | tf_op jit(solution)/shard_map/kcabiq,kabis->kcabqs/dot_general | solution.py:333
  36.0 8.5 %shard_map.78 = f32[4,24,256]{2,1,0:T(8,128)} custom-call(f32[4,24,256]{2,1,0:T(8,128)} %pad_maximum_fusion.6.send_ref), custom_call_target="tpu_custom_call" | custom-call | tf_op jit(solution)/shard_map/pallas_call | solution.py:312
  44.5 0.7 slice_bitcast_fusion.25
  45.2 0.7 slice_bitcast_fusion.30
  46.0 0.8 fusion.114
  47.2 0.7 slice_bitcast_fusion.34
  48.0 1.0 convolution_bitcast_fusion.6
  50.6 0.8 reshape_reshape.15.h_ref
  51.5 22.5 %shard_map.79 = (f32[128,256]{1,0:T(8,128)}, f32[128,256]{1,0:T(8,128)}, f32[128,256]{1,0:T(8,128)}, f32[8,128]{1,0:T(8,128)}) custom-call(f32[128,256]{1,0:T(8,128)} %neg.91.d_ref.r_ref, f32[128,256]{1,0:T(8,128)} %reshape_reshape.15.h_ref, f32[128,256]{1,0:T(8,128)} %neg.91.d_ref.r_ref), custom_call_target="tpu_custom_call" | custom-call | tf_op jit(solution)/shard_map/pallas_call | solution.py:156
  74.0 1.1 reshape_reshape.16
  75.1 0.7 slice.614
  77.2 1.1 fusion.5
  79.7 6.4 %shard_map.80 = f32[4,24,256]{2,1,0:T(8,128)} custom-call(f32[4,24,256]{2,1,0:T(8,128)} %pad_maximum_fusion.7.send_ref), custom_call_target="tpu_custom_call" | custom-call | tf_op jit(solution)/shard_map/pallas_call | solution.py:312
  86.1 0.7 slice_bitcast_fusion.23
  86.8 0.7 slice_bitcast_fusion.29
  87.5 0.7 slice_bitcast_fusion.38
  88.4 0.7 fusion.113
  89.3 0.7 slice_bitcast_fusion.33
  90.2 1.0 convolution_bitcast_fusion.5
  92.6 0.8 reshape_reshape.17.h_ref
  93.5 19.2 %shard_map.81 = (f32[128,256]{1,0:T(8,128)}, f32[128,256]{1,0:T(8,128)}, f32[128,256]{1,0:T(8,128)}, f32[8,128]{1,0:T(8,128)}) custom-call(f32[128,256]{1,0:T(8,128)} %get-tuple-element.12.d_ref, f32[128,256]{1,0:T(8,128)} %reshape_reshape.17.h_ref, f32[128,256]{1,0:T(8,128)} %get-tuple-element.13.r_ref, f32[128,256]{1,0:T(8,128)} %get-tuple-element.14.refs_0_, ...), custom_call_target="tpu_custom_call" | custom-call | tf_op jit(solution)/shard_map/pallas_call | solution.py:156
  112.7 1.1 reshape_reshape.18
  113.8 0.7 slice.642
  115.9 1.1 fusion.4
  118.4 6.4 %shard_map.82 = f32[4,24,256]{2,1,0:T(8,128)} custom-call(f32[4,24,256]{2,1,0:T(8,128)} %pad_maximum_fusion.8.send_ref), custom_call_target="tpu_custom_call" | custom-call | tf_op jit(solution)/shard_map/pallas_call | solution.py:312
  124.8 0.7 slice_bitcast_fusion.21
  125.5 0.7 slice_bitcast_fusion.28
  126.2 0.7 slice_bitcast_fusion.37
  127.1 0.7 fusion.112
  128.0 0.7 slice_bitcast_fusion.32
  128.9 1.0 convolution_bitcast_fusion.4
  131.3 0.8 reshape_reshape.19.h_ref
  132.2 20.8 %shard_map.83 = (f32[128,256]{1,0:T(8,128)}, f32[128,256]{1,0:T(8,128)}) custom-call(f32[128,256]{1,0:T(8,128)} %get-tuple-element.16.d_ref, f32[128,256]{1,0:T(8,128)} %reshape_reshape.19.h_ref, f32[128,256]{1,0:T(8,128)} %get-tuple-element.17.r_ref, f32[128,256]{1,0:T(8,128)} %get-tuple-element.18.refs_0_, f32[8,128]{1,0:T(8,128)} %get-tuple-element.19.refs_1_), custom_call_target="tpu_custom_call" | custom-call | tf_op jit(solution)/shard_map/pallas_call | solution.py:156
  153.0 1.6 %add.434 = f32[2,64,256]{2,1,0:T(8,128)} add(f32[2,64,256]{2,1,0:T(8,128)S(1)} %copy-done, f32[2,64,256]{2,1,0:T(8,128)} %bitcast.559) | non-fusion elementwise | flops 32768 | bytes 393216 | tf_op jit(solution)/shard_map/add | solution.py:434
  154.5 1.6 %copy.842 = f32[2,64,256]{2,1,0:T(8,128)} copy(f32[2,64,256]{2,1,0:T(8,128)} %bitcast.560) | data formatting | bytes 262144
  (313 shorter events, 22.8 us)
Async XLA Ops:
  2.7 0.8 copy-start.10
  4.6 1.3 copy-start.9
  4.9 1.1 copy-start.11
  6.1 0.8 copy-start.12
  7.4 20.4 %copy-start.1 = (f32[1,2,8,32,256]{4,3,2,1,0:T(8,128)}, f32[1,2,8,32,256]{4,3,2,1,0:T(8,128)S(1)}, u32[]{:S(2)}) copy-start(f32[1,2,8,32,256]{4,3,2,1,0:T(8,128)S(1)} %get-tuple-element.141) | copy-start | bytes 1572868
  7.5 0.9 copy-start.13
  7.5 1.0 copy-start.14
  7.8 20.0 %copy-start.3 = (f32[1,2,8,32,256]{4,3,2,1,0:T(8,128)}, f32[1,2,8,32,256]{4,3,2,1,0:T(8,128)S(1)}, u32[]{:S(2)}) copy-start(f32[1,2,8,32,256]{4,3,2,1,0:T(8,128)S(1)} %get-tuple-element.142) | copy-start | bytes 1572868
  7.8 20.0 %copy-start.5 = (f32[1,2,8,32,256]{4,3,2,1,0:T(8,128)}, f32[1,2,8,32,256]{4,3,2,1,0:T(8,128)S(1)}, u32[]{:S(2)}) copy-start(f32[1,2,8,32,256]{4,3,2,1,0:T(8,128)S(1)} %get-tuple-element.143) | copy-start | bytes 1572868
  9.5 0.7 copy-start.24
  10.4 0.5 copy-start.20
  11.3 24.0 %copy-start.17 = (f32[6]{0:T(128)}, f32[6]{0:T(128)S(1)}, u32[]{:S(2)}) copy-start(f32[6]{0:T(128)S(1)} %pad.234.clone) | copy-start | bytes 76
  31.7 1.0 copy-start.2
  31.7 1.2 copy-start.4
  32.9 2.2 %copy-start.21 = (f32[24]{0:T(128)S(1)}, f32[24]{0:T(128)}, u32[]{:S(2)}) copy-start(f32[24]{0:T(128)} %copy-done.20) | copy-start | bytes 292
  45.9 2.1 %copy-start.6 = (f32[1,2,8,32,256]{4,3,2,1,0:T(8,128)S(1)}, f32[1,2,8,32,256]{4,3,2,1,0:T(8,128)}, u32[]{:S(2)}) copy-start(f32[1,2,8,32,256]{4,3,2,1,0:T(8,128)} %copy-done.5) | copy-start | bytes 1572868
  76.0 1.0 copy-start.7
  76.3 0.9 copy-start.15
  77.2 1.2 copy-start.22
  78.3 0.7 copy-start.18
  114.7 1.0 copy-start.8
  115.0 0.9 copy-start.16
  115.9 1.2 copy-start.23
  117.0 0.7 copy-start.19
  131.3 21.6 %copy-start = (f32[2,64,256]{2,1,0:T(8,128)S(1)}, f32[2,64,256]{2,1,0:T(8,128)}, u32[]{:S(2)}) copy-start(f32[2,64,256]{2,1,0:T(8,128)} %param.6) | copy-start | bytes 393220

commit v6 on v5

--- a/solution.py
+++ b/solution.py
@@ -19,10 +19,12 @@
 MESH_ID = pl.DeviceIdType.MESH
 
 
-def _cg_kernel(names, first, last, d_ref, h_ref, r_ref, *refs):
-    if not first:
-        u_ref, rr_ref = refs[:2]
-        refs = refs[2:]
+def _cg_kernel(names, first, last, d_ref, h_ref, *refs):
+    if first:
+        r_ref = d_ref
+    else:
+        r_ref, u_ref, rr_ref = refs[:3]
+        refs = refs[3:]
     if last:
         u_out, r_out, row_buf, col_buf, mine, part, row_send, row_recv, col_send, col_recv = refs
     else:
@@ -146,9 +148,9 @@
     last = iteration == ITERS - 1
     shape = direction.shape
     flat = (shape[0] * shape[1], shape[2])
-    fields = [x.reshape(flat) for x in (direction, image, residual)]
+    fields = [x.reshape(flat) for x in (direction, image)]
     if not first:
-        fields += [update.reshape(flat), norm_tile]
+        fields += [residual.reshape(flat), update.reshape(flat), norm_tile]
     field_type = jax.ShapeDtypeStruct(flat, jnp.float32)
     out_shape = [field_type, field_type]
     if not last:

time: 158 us -> 158 us (level)
  no operation moved by 1% of the time
where the time goes in v6:
time: 158 us; the launch traced here: 156 us
  Pallas kernels  95.2 us (60%)
  local copies, waits for them, and re-layouts  38.6 us (24%)
  other arithmetic  10.9 us (7%)
  matrix products  9.21 us (6%)
  between operations  2.15 us (1%)
    pallas_call x3, Pallas kernels, cg_step(): pl.pallas_call(functools.partial(_cg_kernel, names, first, last), out_sha...  62.3 us
    pallas_call x4, Pallas kernels, halo_exchange(): pl.pallas_call(functools.partial(_halo_kernel, names), out_shape=jax.Shap...  32.8 us
    unnamed x99, local copies, waits for them, and re-layouts  11.4 us
    dot_general x4, matrix products, seam_term(): jnp.einsum('kcabiq,kabis->kcabqs', bands, along_table, precision=lax.Prec...  5.38 us
    dot_general x4, matrix products, seam_term(): jnp.einsum('kcabqs,kabis->kcabiq', weighted, along_table, precision=lax.P...  3.83 us

profile of v6, /device:TPU:1, one launch (start us, length us, event | category | flops | bytes accessed | tf_op | source)
XLA Modules:
  0.0 156.0 jit_solution(1659074264635442861)
XLA Ops:
  0.6 1.1 reshape.848
  3.6 0.7 slice.535
  5.1 0.7 slice.532
  8.5 1.1 fusion.7
  11.4 0.7 pad_maximum_fusion.5.send_ref
  12.0 11.6 %shard_map.77 = f32[4,24,256]{2,1,0:T(8,128)} custom-call(f32[4,24,256]{2,1,0:T(8,128)} %pad_maximum_fusion.5.send_ref), custom_call_target="tpu_custom_call" | custom-call | tf_op jit(solution)/shard_map/pallas_call | solution.py:314
  23.6 0.7 slice_bitcast_fusion.27
  24.3 0.7 slice_bitcast_fusion.31
  25.0 0.7 slice_bitcast_fusion.39
  25.8 0.7 fusion.115
  26.8 0.7 slice_bitcast_fusion.35
  27.8 1.0 convolution_bitcast_fusion.7
  30.5 0.8 neg.91.d_ref
  32.9 2.1 %fusion.6 = f32[4,2,2,8,256]{4,1,3,2,0:T(2,128)S(1)} fusion(f32[1,2,2,8,32,4]{4,5,1,3,2,0:T(4,128)S(1)} %get-tuple-element.33, f32[1,2,2,8,32,4]{4,5,1,3,2,0:T(4,128)S(1)} %bitcast.590, f32[1,2,2,8,32,4]{4,5,1,3,2,0:T(4,128)S(1)} %bitcast.574, f32[1,2,2,8,32,4]{4,5,1,3,2,0:T(4,128)S(1)} %bitcast.593, f32[4,2,8,4,256]{4,3,2,1,0:T(4,128)S(1)} %pad_maximum_fusion, ...), kind=kOutput, calls=%fused_computation.11 | convolution fusion | flops 27017216 | bytes 2555904 | tf_op jit(solution)/shard_map/kcabiq,kabis->kcabqs/dot_general | solution.py:335
  36.0 8.5 %shard_map.78 = f32[4,24,256]{2,1,0:T(8,128)} custom-call(f32[4,24,256]{2,1,0:T(8,128)} %pad_maximum_fusion.6.send_ref), custom_call_target="tpu_custom_call" | custom-call | tf_op jit(solution)/shard_map/pallas_call | solution.py:314
  44.5 0.7 slice_bitcast_fusion.25
  45.2 0.7 slice_bitcast_fusion.30
  46.0 0.8 fusion.114
  47.2 0.7 slice_bitcast_fusion.34
  48.0 1.0 convolution_bitcast_fusion.6
  50.6 0.8 reshape_reshape.15.h_ref
  51.5 22.4 %shard_map.79 = (f32[128,256]{1,0:T(8,128)}, f32[128,256]{1,0:T(8,128)}, f32[128,256]{1,0:T(8,128)}, f32[8,128]{1,0:T(8,128)}) custom-call(f32[128,256]{1,0:T(8,128)} %neg.91.d_ref, f32[128,256]{1,0:T(8,128)} %reshape_reshape.15.h_ref), custom_call_target="tpu_custom_call" | custom-call | tf_op jit(solution)/shard_map/pallas_call | solution.py:158
  73.9 1.1 reshape_reshape.16
  75.1 0.7 slice.614
  77.1 1.1 fusion.5
  79.6 6.4 %shard_map.80 = f32[4,24,256]{2,1,0:T(8,128)} custom-call(f32[4,24,256]{2,1,0:T(8,128)} %pad_maximum_fusion.7.send_ref), custom_call_target="tpu_custom_call" | custom-call | tf_op jit(solution)/shard_map/pallas_call | solution.py:314
  86.0 0.7 slice_bitcast_fusion.23
  86.7 0.7 slice_bitcast_fusion.29
  87.4 0.7 slice_bitcast_fusion.38
  88.3 0.7 fusion.113
  89.2 0.7 slice_bitcast_fusion.33
  90.2 1.0 convolution_bitcast_fusion.5
  92.6 0.8 reshape_reshape.17.h_ref
  93.4 19.2 %shard_map.81 = (f32[128,256]{1,0:T(8,128)}, f32[128,256]{1,0:T(8,128)}, f32[128,256]{1,0:T(8,128)}, f32[8,128]{1,0:T(8,128)}) custom-call(f32[128,256]{1,0:T(8,128)} %get-tuple-element.12.d_ref, f32[128,256]{1,0:T(8,128)} %reshape_reshape.17.h_ref, f32[128,256]{1,0:T(8,128)} %get-tuple-element.13.refs_0_, f32[128,256]{1,0:T(8,128)} %get-tuple-element.14.refs_1_, ...), custom_call_target="tpu_custom_call" | custom-call | tf_op jit(solution)/shard_map/pallas_call | solution.py:158
  112.6 1.1 reshape_reshape.18
  113.7 0.7 slice.642
  115.8 1.1 fusion.4
  118.3 6.4 %shard_map.82 = f32[4,24,256]{2,1,0:T(8,128)} custom-call(f32[4,24,256]{2,1,0:T(8,128)} %pad_maximum_fusion.8.send_ref), custom_call_target="tpu_custom_call" | custom-call | tf_op jit(solution)/shard_map/pallas_call | solution.py:314
  124.7 0.7 slice_bitcast_fusion.21
  125.4 0.7 slice_bitcast_fusion.28
  126.1 0.7 slice_bitcast_fusion.37
  127.0 0.7 fusion.112
  127.9 0.7 slice_bitcast_fusion.32
  128.9 1.0 convolution_bitcast_fusion.4
  131.3 0.8 reshape_reshape.19.h_ref
  132.1 20.8 %shard_map.83 = (f32[128,256]{1,0:T(8,128)}, f32[128,256]{1,0:T(8,128)}) custom-call(f32[128,256]{1,0:T(8,128)} %get-tuple-element.16.d_ref, f32[128,256]{1,0:T(8,128)} %reshape_reshape.19.h_ref, f32[128,256]{1,0:T(8,128)} %get-tuple-element.17.refs_0_, f32[128,256]{1,0:T(8,128)} %get-tuple-element.18.refs_1_, f32[8,128]{1,0:T(8,128)} %get-tuple-element.19.refs_2_), custom_call_target="tpu_custom_call" | custom-call | tf_op jit(solution)/shard_map/pallas_call | solution.py:158
  152.9 1.6 %add.434 = f32[2,64,256]{2,1,0:T(8,128)} add(f32[2,64,256]{2,1,0:T(8,128)S(1)} %copy-done, f32[2,64,256]{2,1,0:T(8,128)} %bitcast.559) | non-fusion elementwise | flops 32768 | bytes 393216 | tf_op jit(solution)/shard_map/add | solution.py:436
  154.5 1.6 %copy.842 = f32[2,64,256]{2,1,0:T(8,128)} copy(f32[2,64,256]{2,1,0:T(8,128)} %bitcast.560) | data formatting | bytes 262144
  (313 shorter events, 22.8 us)
Async XLA Ops:
  2.7 0.8 copy-start.10
  4.6 1.3 copy-start.9
  4.9 1.1 copy-start.11
  6.1 0.8 copy-start.12
  7.4 20.4 %copy-start.1 = (f32[1,2,8,32,256]{4,3,2,1,0:T(8,128)}, f32[1,2,8,32,256]{4,3,2,1,0:T(8,128)S(1)}, u32[]{:S(2)}) copy-start(f32[1,2,8,32,256]{4,3,2,1,0:T(8,128)S(1)} %get-tuple-element.141) | copy-start | bytes 1572868
  7.5 0.9 copy-start.13
  7.5 1.0 copy-start.14
  7.8 20.0 %copy-start.3 = (f32[1,2,8,32,256]{4,3,2,1,0:T(8,128)}, f32[1,2,8,32,256]{4,3,2,1,0:T(8,128)S(1)}, u32[]{:S(2)}) copy-start(f32[1,2,8,32,256]{4,3,2,1,0:T(8,128)S(1)} %get-tuple-element.142) | copy-start | bytes 1572868
  7.8 20.0 %copy-start.5 = (f32[1,2,8,32,256]{4,3,2,1,0:T(8,128)}, f32[1,2,8,32,256]{4,3,2,1,0:T(8,128)S(1)}, u32[]{:S(2)}) copy-start(f32[1,2,8,32,256]{4,3,2,1,0:T(8,128)S(1)} %get-tuple-element.143) | copy-start | bytes 1572868
  9.5 0.7 copy-start.24
  10.4 0.5 copy-start.20
  11.3 24.0 %copy-start.17 = (f32[6]{0:T(128)}, f32[6]{0:T(128)S(1)}, u32[]{:S(2)}) copy-start(f32[6]{0:T(128)S(1)} %pad.234.clone) | copy-start | bytes 76
  31.7 1.0 copy-start.2
  31.7 1.2 copy-start.4
  32.9 2.2 %copy-start.21 = (f32[24]{0:T(128)S(1)}, f32[24]{0:T(128)}, u32[]{:S(2)}) copy-start(f32[24]{0:T(128)} %copy-done.20) | copy-start | bytes 292
  45.9 2.1 %copy-start.6 = (f32[1,2,8,32,256]{4,3,2,1,0:T(8,128)S(1)}, f32[1,2,8,32,256]{4,3,2,1,0:T(8,128)}, u32[]{:S(2)}) copy-start(f32[1,2,8,32,256]{4,3,2,1,0:T(8,128)} %copy-done.5) | copy-start | bytes 1572868
  76.0 1.0 copy-start.7
  76.3 0.9 copy-start.15
  77.1 1.2 copy-start.22
  78.2 0.7 copy-start.18
  114.6 1.0 copy-start.8
  114.9 0.9 copy-start.16
  115.8 1.2 copy-start.23
  116.9 0.7 copy-start.19
  131.3 21.6 %copy-start = (f32[2,64,256]{2,1,0:T(8,128)S(1)}, f32[2,64,256]{2,1,0:T(8,128)}, u32[]{:S(2)}) copy-start(f32[2,64,256]{2,1,0:T(8,128)} %param.6) | copy-start | bytes 393220
